TPU v7x, 256 devices: a whole 4x4x8 slice. The times are simulated.
256 devices in a mesh: gx: 32 (over z, x), gy: 4 (over y), gz: 2 (over core).
Axes of the slice: x: 4, y: 4, z: 8, core: 2. Of those that a mesh axis runs over, the one named last changes fastest.
Arguments:
- viscosity: bfloat16 [8, 2048, 1024], P('gz', 'gx', 'gy'), may hold values from 0.29882812 to 3
- velocity: bfloat16 [2, 8, 2048, 1024], P(None, 'gz', 'gx', 'gy'), may hold values from -6 to 6
- log_friction: float32 [2048, 1024], P('gx', 'gy'), may hold values from -1 to 1
- step_dir: float32 [2048, 1024], P('gx', 'gy'), may hold values from -6 to 6
- obs_weight: float32 [2048, 1024], P('gx', 'gy'), may hold values from 1 to 8
- tile_mask: int32 [32, 16], P('gx', 'gy'), may hold values from 0 to 2
- contact: int32 [2048, 1024], P('gx', 'gy'), may hold values 0 or 1
Outputs:
- depth_response: float32 [2, 2048, 1024], P(None, 'gx', 'gy')
- hess_vec: float32 [2048, 1024], P('gx', ('gy', 'gz'))
Inputs may be any that keep to these rules, and one draw needn't show every extreme that they name: `tile_mask`: each tile's class: 0 ocean, 1 floating ice, 2 grounded ice.
All inputs are finite; a program needn't handle non-finite values. No bound on the sum of `contact` on one device may be relied on, other than what follows from the above.
Results may differ from a plain program's by a relative error of at most 0.0024.
Values may be sent and summed in bfloat16 or wider, within the bound.
A program may use at most 64 MiB of HBM per device.

v0:
```python
import jax
import jax.numpy as jnp
from jax import lax
from jax.sharding import PartitionSpec as P

ITERS = 8
SWEEPS = 2
TILE = 64


ASPECT = 16.0
LOWER = 0.1
UPPER = 2.0


def extended(cells, sides, width):
    for axis, dim in sides:
        count = lax.axis_size(axis)
        ends = count - 1
        head = lax.slice_in_dim(cells, 0, width, axis=dim)
        tail = lax.slice_in_dim(cells, cells.shape[dim] - width, cells.shape[dim], axis=dim)
        cells = jnp.concatenate(
            [
                lax.ppermute(tail, axis, [(i, (i + 1) % count) for i in range(ends)]),
                cells,
                lax.ppermute(head, axis, [((i + 1) % count, i) for i in range(ends)]),
            ],
            axis=dim,
        )
    return cells


def shifted_2(value, axis, by):
    size = lax.axis_size(axis)
    pairs = [(i, i + by) for i in range(size) if 0 <= i + by < size]
    return lax.ppermute(value, axis, pairs)


def expand(tiles):
    return jnp.repeat(jnp.repeat(tiles, TILE, axis=0), TILE, axis=1)


def coefficients(values):
    center_eta = values[1:-1, 1:-1, 1:-1]

    def flat(beside):
        return jnp.where(beside > 0, 0.5 * (center_eta + beside), center_eta)

    def vertical(beside):
        return jnp.where(
            beside > 0, ASPECT * 0.5 * (center_eta + beside), jnp.zeros_like(center_eta)
        )

    return (
        flat(values[1:-1, :-2, 1:-1]),
        flat(values[1:-1, 2:, 1:-1]),
        flat(values[1:-1, 1:-1, :-2]),
        flat(values[1:-1, 1:-1, 2:]),
        vertical(values[:-2, 1:-1, 1:-1]),
        vertical(values[2:, 1:-1, 1:-1]),
    )


def stencil(padded, face_terms, diagonal, ice_cells):
    shifted_all = (
        padded[:, 1:-1, :-2, 1:-1],
        padded[:, 1:-1, 2:, 1:-1],
        padded[:, 1:-1, 1:-1, :-2],
        padded[:, 1:-1, 1:-1, 2:],
        padded[:, :-2, 1:-1, 1:-1],
        padded[:, 2:, 1:-1, 1:-1],
    )
    beside = face_terms[0] * shifted_all[0].astype(jnp.float32)
    for factor, shifted in zip(face_terms[1:], shifted_all[1:]):
        beside = beside + factor * shifted.astype(jnp.float32)
    center = padded[:, 1:-1, 1:-1, 1:-1].astype(jnp.float32)
    return ice_cells * (diagonal * center - beside) + (1.0 - ice_cells) * center


def chebyshev(operator, inverse_diag, forcing):
    centre_value = (UPPER + LOWER) / 2.0
    half_width = (UPPER - LOWER) / 2.0
    sigma_ratio = centre_value / half_width
    solution = jnp.zeros(forcing.shape, jnp.float32)
    for sweep_index in range(SWEEPS):
        if sweep_index == 0:
            residual = forcing
        else:
            residual = forcing - operator(solution.astype(jnp.bfloat16))
        direction = inverse_diag * residual / centre_value
        rho_now = 1.0 / sigma_ratio
        for iter_index in range(ITERS):
            solution = solution + direction
            if iter_index + 1 < ITERS:
                residual = residual - operator(direction.astype(jnp.bfloat16))
                rho_next = 1.0 / (2.0 * sigma_ratio - rho_now)
                direction = (
                    rho_next * rho_now * direction
                    + 2.0 * rho_next / half_width * inverse_diag * residual
                )
                rho_now = rho_next
    return solution


def per_device(viscosity, velocity, log_friction, step_dir, obs_weight, tile_mask, contact):
    ice_cells = expand(tile_mask > 0).astype(jnp.float32)
    grounded = expand(tile_mask == 2).astype(jnp.float32)
    friction = jnp.exp(log_friction) * grounded * contact.astype(jnp.float32)
    half_cols = log_friction.shape[1] // 2
    stacked = viscosity[None]

    def with_rims(field):
        return extended(field, (("gx", 2), ("gy", 3), ("gz", 1)), 1)

    layers = stacked.shape[1]
    lowest = jnp.logical_and(jnp.arange(layers) == 0, lax.axis_index("gz") == 0)
    bottom = lowest.astype(jnp.float32)[:, None, None]
    values = with_rims(stacked)[0].astype(jnp.float32)
    face_terms = coefficients(values)
    diagonal = (
        face_terms[0]
        + face_terms[1]
        + face_terms[2]
        + face_terms[3]
        + face_terms[4]
        + face_terms[5]
        + friction * bottom
    )
    inverse_diag = ice_cells / diagonal + (1.0 - ice_cells)

    def operator(field):
        return stencil(with_rims(field), face_terms, diagonal, ice_cells)

    u_base = velocity[:, 0].astype(jnp.float32)
    forcing = (-(friction * step_dir) * u_base)[:, None] * bottom
    response = chebyshev(operator, inverse_diag, forcing)
    column_sum = jnp.sum(response, axis=1)
    depth_local = lax.psum(column_sum, "gz")
    adjoint_rhs = jnp.broadcast_to((ice_cells * obs_weight * depth_local)[:, None], response.shape)
    multiplier = chebyshev(operator, inverse_diag, adjoint_rhs)
    basal = -friction * jnp.sum(u_base * multiplier[:, 0], axis=0)
    upper_half = shifted_2(basal[:, half_cols:], "gz", 1)
    hess_vec = jnp.where(lax.axis_index("gz") == 0, basal[:, :half_cols], upper_half)
    return (depth_local, hess_vec)


def solution(mesh):
    in_specs = (
        P("gz", "gx", "gy"),
        P(None, "gz", "gx", "gy"),
        P("gx", "gy"),
        P("gx", "gy"),
        P("gx", "gy"),
        P("gx", "gy"),
        P("gx", "gy"),
    )
    out_specs = (P(None, "gx", "gy"), P("gx", ("gy", "gz")))
    return jax.shard_map(
        per_device, mesh=mesh, in_specs=in_specs, out_specs=out_specs, check_vma=False
    )
```

profile of v0, /device:TPU:103, one launch (start us, length us, event | category | flops | bytes accessed | tf_op | source)
XLA Modules:
  0.0 866.0 jit_solution(4809203129304106115)
XLA Ops:
  30.2 5.4 collective-permute-start.5
  59.5 5.1 collective-permute-start.11
  86.8 4.9 collective-permute-start.17
  112.6 4.9 collective-permute-start.23
  138.4 4.9 collective-permute-start.29
  164.2 4.9 collective-permute-start.35
  189.9 4.9 collective-permute-start.41
  215.7 4.9 collective-permute-start.47
  242.7 4.9 collective-permute-start.53
  268.4 4.9 collective-permute-start.59
  294.2 4.9 collective-permute-start.65
  319.9 4.9 collective-permute-start.71
  345.7 4.9 collective-permute-start.77
  371.5 4.9 collective-permute-start.83
  397.3 4.9 collective-permute-start.89
  423.0 4.9 collective-permute-start.95
  432.7 24.6 %all-reduce.2.cloned.1.call-done = f32[2,64,256]{2,1,0:T(8,128)} async-done(((f32[2,64,256]{2,1,0:T(8,128)}), f32[2,64,256]{2,1,0:T(8,128)}) %all-reduce.2.cloned.1.call-update) | async-done | bytes 131088 | tf_op jit(solution)/shard_map/psum | solution.py:138
  464.5 5.8 collective-permute-done.97
  481.0 5.0 collective-permute-start.101
  508.5 4.9 collective-permute-start.107
  535.5 4.9 collective-permute-start.113
  561.3 4.9 collective-permute-start.119
  587.1 4.9 collective-permute-start.125
  612.8 4.9 collective-permute-start.131
  638.7 4.9 collective-permute-start.137
  665.9 4.9 collective-permute-start.143
  691.9 4.9 collective-permute-start.149
  717.7 4.9 collective-permute-start.155
  743.5 4.9 collective-permute-start.161
  769.2 4.9 collective-permute-start.167
  795.0 4.9 collective-permute-start.173
  820.7 4.9 collective-permute-start.179
  (543 shorter events, 671.9 us)
Async XLA Ops:
  7.2 450.0 %all-reduce.2.cloned.1.call-start = ((), (), s32[]{:S(2)}) async-start(), calls=%async_computation | async-start | bytes 262144 | tf_op jit(solution)/shard_map/psum | solution.py:138
  8.0 8.8 %collective-permute-start = (bf16[1,4,1,256]{3,2,1,0:T(2,128)(2,1)S(1)}, bf16[1,4,1,256]{3,2,1,0:T(2,128)(2,1)S(1)}, u32[]{:S(2)}, u32[]{:S(2)}) collective-permute-start(bf16[1,4,1,256]{3,2,1,0:T(2,128)(2,1)S(1)} %get-tuple-element.274), channel_id=1, source_target_pairs={{0,8},{8,16},{16,24},{24,32},{32,40},{40,48},{48,56},{56,64},{64,7... | collective-permute-start | bytes 6152 | tf_op jit(solution)/shard_map/ppermute | solution.py:24
  40.9 7.7 collective-permute-start.7
  68.6 7.7 collective-permute-start.13
  95.7 7.7 collective-permute-start.19
  121.4 7.7 collective-permute-start.25
  147.2 7.7 collective-permute-start.31
  173.0 7.7 collective-permute-start.37
  198.8 7.7 collective-permute-start.43
  225.7 7.7 collective-permute-start.49
  251.5 7.7 collective-permute-start.55
  277.3 7.7 collective-permute-start.61
  303.0 7.7 collective-permute-start.67
  328.8 7.7 collective-permute-start.73
  354.5 7.7 collective-permute-start.79
  380.3 7.7 collective-permute-start.85
  406.1 7.7 collective-permute-start.91
  462.6 7.7 collective-permute-start.97
  490.0 7.7 collective-permute-start.103
  517.4 7.7 collective-permute-start.109
  544.3 7.7 collective-permute-start.115
  570.1 7.7 collective-permute-start.121
  595.9 7.7 collective-permute-start.127
  621.7 7.7 collective-permute-start.133
  649.0 7.7 collective-permute-start.139
  674.7 7.7 collective-permute-start.145
  700.8 7.7 collective-permute-start.151
  726.5 7.7 collective-permute-start.157
  752.3 7.7 collective-permute-start.163
  778.0 7.7 collective-permute-start.169
  803.8 7.7 collective-permute-start.175
  829.5 7.7 collective-permute-start.181
  (166 other events, 1695.9 us)
Sparse Core Ops, SparseCore 0:
  432.0 25.2 all-reduce.1
where the time goes:
time: 880 us; the launch traced here: 866 us
  starting transfers between devices  460 us (52%)
  waiting for transfers between devices  331 us (38%)
  other arithmetic  51.4 us (6%)
  between operations  17.1 us (2%)
    ppermute x93, starting transfers between devices, extended(): lax.ppermute(head, axis, [((i + 1) % count, i) for i in range(ends)])  294 us
    ppermute x93, waiting for transfers between devices, extended(): lax.ppermute(head, axis, [((i + 1) % count, i) for i in range(ends)])  282 us
    ppermute x93, starting transfers between devices, extended(): lax.ppermute(tail, axis, [(i, (i + 1) % count) for i in range(ends)])  165 us
    convert_element_type x27, other arithmetic, chebyshev(): residual = residual - operator(direction.astype(jnp.bfloat16))  26 us
    psum x1, waiting for transfers between devices, per_device(): depth_local = lax.psum(column_sum, 'gz')  24.6 us
    ppermute x93, waiting for transfers between devices, extended(): lax.ppermute(tail, axis, [(i, (i + 1) % count) for i in range(ends)])  22.6 us
  transfers between devices with their start and end apart: 188, of which 126 were waited for; matrix products, arithmetic and copies ran while one was open for 0% of the time, Pallas kernels for 0%

commit v1 on v0

v1 whole, which is shorter than its diff:
```python
import functools
import math

import jax
import jax.numpy as jnp
from jax import lax
from jax.experimental import pallas as pl
from jax.experimental.pallas import tpu as pltpu
from jax.sharding import PartitionSpec as P

MESH = pl.DeviceIdType.MESH
F32 = jnp.float32
BF16 = jnp.bfloat16

SWEEP = 8
ASPECT = 16.0
LOWER = 0.1
UPPER = 2.0
CENTRE = (UPPER + LOWER) / 2.0
HALF = (UPPER - LOWER) / 2.0
SIGMA = CENTRE / HALF

DELTA = CENTRE - 1.0
LINEAR = DELTA + CENTRE
ORDER = (3, 6, 1, 4, 5, 2, 7)
ANGLES = [math.pi * j / SWEEP for j in ORDER]
PS = [2.0 * DELTA - 2.0 * CENTRE * math.cos(t) for t in ANGLES]
QS = [
    DELTA * DELTA - 2.0 * CENTRE * DELTA * math.cos(t) + CENTRE * CENTRE - (HALF * math.sin(t)) ** 2
    for t in ANGLES
]
TOP = math.cosh(SWEEP * math.acosh(SIGMA))
SCALE = 2.0 ** (2 * SWEEP - 2) / (TOP * TOP) / HALF ** (2 * SWEEP)

WIDE = 16
NX, NY, NZ = 64, 128, 8
ROWS = NX // 2 + WIDE
XT = NX + 2 * WIDE
LANES = 4 * (NY + 2 * WIDE)
TILES = LANES // 128
CHUNK = 4
DIRS = [(dx, dy) for dx in (-1, 0, 1) for dy in (-1, 0, 1) if (dx, dy) != (0, 0)]


def lanes_of(shape):
    return lax.broadcasted_iota(jnp.int32, shape, len(shape) - 1)


def turned(value, by):
    by %= 128
    return value if by == 0 else pltpu.roll(value, by, value.ndim - 1)


def triple_low(own, left, right):
    lane = lanes_of(own[0].shape)

    def put(piece, to):
        return turned(piece[0], to - piece[1])

    a, b = turned(own[0], 16), turned(own[1], 48)
    t0 = jnp.where(lane < 16, put(left[0], 0), a)
    t1 = jnp.where(lane < 16, a, jnp.where(lane < 32, put(right[0], 16), jnp.where(lane < 48, put(left[1], 32), b)))
    t2 = jnp.where(lane < 48, b, put(right[1], 48))
    return t0, t1, t2


def triple_high(own, left, right):
    lane = lanes_of(own[0].shape)

    def put(piece, to):
        return turned(piece[0], to - piece[1])

    a, b = turned(own[0], 80), turned(own[1], 112)
    t2 = jnp.where(lane < 80, put(left[0], 64), a)
    t3 = jnp.where(
        lane < 80, a, jnp.where(lane < 96, put(right[0], 80), jnp.where(lane < 112, put(left[1], 96), b))
    )
    t4 = jnp.where(lane < 112, b, put(right[1], 112))
    return t2, t3, t4


def joined_tiles(low, high):
    middle = jnp.where(lanes_of(low[2].shape) < 64, low[2], high[0])
    return jnp.concatenate([low[0], low[1], middle, high[1], high[2]], axis=-1)


def kernel(
    gx_n,
    gy_n,
    visc_ref,
    vel_ref,
    logf_ref,
    step_ref,
    obs_ref,
    contact_ref,
    tile_ref,
    depth_ref,
    hess_ref,
    visc,
    edge_l,
    edge_r,
    pack_l,
    pack_r,
    base,
    logf,
    step,
    obs,
    contact,
    flat,
    flat_pack,
    flat_l,
    flat_r,
    rhs,
    rhs_pack,
    rhs_l,
    rhs_r,
    depth,
    hess,
    vlow,
    vhigh,
    flow,
    fhigh,
    clow,
    chigh,
    dlow,
    dhigh,
    gs,
    inv,
    u_buf,
    t_buf,
    local_sem,
    swap_send,
    swap_recv,
    a_send,
    a_recv,
    b_send,
    b_recv,
    c_send,
    c_recv,
):
    gx, gy, gz = lax.axis_index("gx"), lax.axis_index("gy"), lax.axis_index("gz")
    yb = 2 * gy + gz
    y_n = 2 * gy_n

    def there(dx, dy):
        nx, ny = gx + dx, yb + dy
        return (nx >= 0) & (nx < gx_n) & (ny >= 0) & (ny < y_n)

    def device(dx, dy):
        ny = yb + dy
        return (gx + dx, lax.div(ny, 2), lax.rem(ny, 2))

    own_cols = pl.ds(pl.multiple_of(gz * NY, NY), NY)
    other_cols = pl.ds(pl.multiple_of((1 - gz) * NY, NY), NY)
    own_rows = pl.ds(WIDE, NX)
    layers = visc_ref.shape[0]
    mine = pl.ds(gz * layers, layers)
    partner = (gx, gy, 1 - gz)

    local = [
        pltpu.make_async_copy(visc_ref.at[:, :, own_cols], visc.at[mine, own_rows], local_sem.at[0]),
        pltpu.make_async_copy(vel_ref.at[:, 0, :, own_cols], base.at[gz], local_sem.at[1]),
        pltpu.make_async_copy(logf_ref.at[:, own_cols], logf, local_sem.at[2]),
        pltpu.make_async_copy(step_ref.at[:, own_cols], step, local_sem.at[3]),
        pltpu.make_async_copy(contact_ref.at[:, own_cols], contact, local_sem.at[4]),
        pltpu.make_async_copy(obs_ref.at[:, own_cols], obs, local_sem.at[5]),
    ]
    for copy in local:
        copy.start()

    barrier = pltpu.get_barrier_semaphore()
    met = 0
    for d in DIRS:
        here = there(*d)
        met = met + here.astype(jnp.int32)

        @pl.when(here)
        def _():
            pl.semaphore_signal(barrier, inc=1, device_id=device(*d), device_id_type=MESH)

    @pl.when(gx == 0)
    def _():
        visc[:, 0:WIDE, :] = jnp.zeros((NZ, WIDE, NY), BF16)
        flat[:, 0:WIDE, :] = jnp.zeros((3, WIDE, NY), F32)
        rhs[:, 0:WIDE, :] = jnp.zeros((2, WIDE, NY), F32)

    @pl.when(gx == gx_n - 1)
    def _():
        visc[:, XT - WIDE : XT, :] = jnp.zeros((NZ, WIDE, NY), BF16)
        flat[:, XT - WIDE : XT, :] = jnp.zeros((3, WIDE, NY), F32)
        rhs[:, XT - WIDE : XT, :] = jnp.zeros((2, WIDE, NY), F32)

    for dy, ends in ((-1, (edge_l, flat_l, rhs_l)), (1, (edge_r, flat_r, rhs_r))):
        for dx, first, count in ((-1, 0, WIDE), (0, WIDE, NX), (1, WIDE + NX, WIDE)):

            @pl.when(jnp.logical_not(there(dx, dy)))
            def _():
                for end in ends:
                    end[first : first + count, :] = jnp.zeros((count, 128), end.dtype)

    pl.semaphore_wait(barrier, met)

    swap = [
        pltpu.make_async_remote_copy(
            visc_ref.at[:, :, other_cols],
            visc.at[mine, own_rows],
            swap_send.at[0],
            swap_recv.at[0],
            device_id=partner,
            device_id_type=MESH,
        ),
        pltpu.make_async_remote_copy(
            vel_ref.at[:, 0, :, other_cols],
            base.at[gz],
            swap_send.at[1],
            swap_recv.at[1],
            device_id=partner,
            device_id_type=MESH,
        ),
    ]
    for copy in swap:
        copy.start()

    for copy in local[1:]:
        copy.wait()

    lane = lanes_of((NX, NY))
    left_class, right_class = tile_ref[0, 2 * gz], tile_ref[0, 2 * gz + 1]
    kinds = jnp.where(lane < NY // 2, left_class, right_class)
    ice = (kinds > 0).astype(F32)
    friction = jnp.exp(logf[...]) * (kinds == 2).astype(F32) * contact[...].astype(F32)
    marked = jnp.where(kinds > 0, jnp.maximum(friction, 1e-30), 0.0)
    flat[2, own_rows, :] = marked

    swap[1].wait()
    drive = -(friction * step[...])
    flat[0, own_rows, :] = drive * base[0, 0].astype(F32)
    flat[1, own_rows, :] = drive * base[0, 1].astype(F32)

    fields = [flat[i, own_rows, :] for i in range(3)]
    packed = jnp.zeros((NX, 128), F32)
    for i, field in enumerate(fields):
        packed = jnp.where((lane >= 16 * i) & (lane < 16 * i + 16), turned(field, 16 * i), packed)
        at = 48 + 16 * i
        packed = jnp.where((lane >= at) & (lane < at + 16), turned(field, at - 112), packed)
    flat_pack[...] = packed

    def spread(dx):
        if dx == 0:
            return pl.ds(WIDE, NX), pl.ds(0, NX), pl.ds(WIDE, NX)
        if dx < 0:
            return pl.ds(WIDE, WIDE), pl.ds(0, WIDE), pl.ds(WIDE + NX, WIDE)
        return pl.ds(NX, WIDE), pl.ds(NX - WIDE, WIDE), pl.ds(0, WIDE)

    def to_neighbours(block, packs, lands, send, recv):
        copies = []
        for i, (dx, dy) in enumerate(DIRS):
            src, src_pack, dst = spread(dx)
            if dy == 0:
                pair = (block.at[:, src, :], block.at[:, dst, :])
            elif dy < 0:
                pair = (packs[0].at[src_pack, :], lands[1].at[dst, :])
            else:
                pair = (packs[1].at[src_pack, :], lands[0].at[dst, :])
            copies.append(
                pltpu.make_async_remote_copy(
                    *pair,
                    send.at[i],
                    recv.at[i],
                    device_id=device(dx, dy),
                    device_id_type=MESH,
                )
            )
        return copies

    def start_all(copies):
        for (dx, dy), copy in zip(DIRS, copies):
            pl.when(there(dx, dy))(copy.start)

    def arrived(copies):
        for (dx, dy), copy in zip(DIRS, copies):
            pl.when(there(-dx, -dy))(copy.wait_recv)

    def sent(copies):
        for (dx, dy), copy in zip(DIRS, copies):
            pl.when(there(dx, dy))(copy.wait_send)

    flat_copies = to_neighbours(flat, (flat_pack, flat_pack), (flat_l, flat_r), b_send, b_recv)
    start_all(flat_copies)

    local[0].wait()
    swap[0].wait()

    def pack_rows(i, _):
        rows = pl.ds(pl.multiple_of(i * 16, 16), 16)
        here = pl.ds(pl.multiple_of(WIDE + i * 16, 16), 16)
        spot = lanes_of((16, 128))
        low = jnp.zeros((16, 128), F32)
        high = jnp.zeros((16, 128), F32)
        for layer in range(NZ):
            e = visc[layer, here, :].astype(F32)
            inside = (spot >= 16 * layer) & (spot < 16 * layer + 16)
            low = jnp.where(inside, turned(e, 16 * layer), low)
            high = jnp.where(inside, turned(e, 16 * layer + 16), high)
        pack_l[rows, :] = low.astype(BF16)
        pack_r[rows, :] = high.astype(BF16)
        return 0

    lax.fori_loop(0, NX // 16, pack_rows, 0)
    visc_copies = to_neighbours(visc, (pack_l, pack_r), (edge_l, edge_r), a_send, a_recv)
    start_all(visc_copies)

    arrived(flat_copies)
    arrived(visc_copies)

    def spread_rows(i, _):
        for half, (place, out) in enumerate(((triple_low, vlow), (triple_high, vhigh))):
            rows = pl.ds(pl.multiple_of(half * ROWS + i * 16, 16), 16)
            ends_l, ends_r = edge_l[rows, :].astype(F32), edge_r[rows, :].astype(F32)
            for layer in range(NZ):
                own = visc[layer, rows, :].astype(F32)
                lefts, rights = (ends_l, 16 * layer), (ends_r, 16 * layer)
                for j, tile in enumerate(place((own, own), (lefts, lefts), (rights, rights))):
                    out[j, pl.ds(i * 16 * NZ + layer, 16, stride=NZ), :] = tile
        return 0

    lax.fori_loop(0, ROWS // 16, spread_rows, 0)

    def eight(i):
        return pl.ds(pl.multiple_of(i * NZ, NZ), NZ)

    t_buf[0] = jnp.zeros((NZ, LANES), F32)
    u_buf[0] = jnp.zeros((NZ, LANES), F32)

    def join_row(q, _):
        low = [vlow[j, eight(q), :] for j in range(3)]
        high = [vhigh[j, eight(ROWS - 1 - q), :] for j in range(3)]
        t_buf[q + 1] = joined_tiles(low, high)
        return 0

    lax.fori_loop(0, ROWS, join_row, 0)

    def close(buf):
        buf[ROWS + 1] = pltpu.roll(buf[ROWS], LANES // 2, 1)

    close(t_buf)

    def assemble(own, which, ends_l, ends_r, spots_l, spots_r, outs):
        def body(i, _):
            for half, (place, out) in enumerate(((triple_low, outs[0]), (triple_high, outs[1]))):
                rows = pl.ds(pl.multiple_of(half * ROWS + i * 8, 8), 8)
                l, r = ends_l[rows, :], ends_r[rows, :]
                pieces = [own[k, rows, :] for k in which]
                tiles = place(pieces, [(l, s) for s in spots_l], [(r, s) for s in spots_r])
                for j, tile in enumerate(tiles):
                    out[j, pl.ds(pl.multiple_of(i * 8, 8), 8), :] = tile
            return 0

        lax.fori_loop(0, ROWS // 8, body, 0)

    def flat_row(low, high, q):
        one = [low[j, pl.ds(q, 1), :] for j in range(3)]
        two = [high[j, pl.ds(ROWS - 1 - q, 1), :] for j in range(3)]
        return jnp.broadcast_to(joined_tiles(one, two), (NZ, LANES))

    assemble(flat, (2, 2), flat_l, flat_r, (80, 80), (32, 32), (clow, chigh))
    assemble(flat, (0, 1), flat_l, flat_r, (48, 64), (0, 16), (flow, fhigh))

    level = lax.broadcasted_iota(jnp.int32, (NZ, LANES), 0)

    def faces(q, _):
        here = t_buf[q + 1]

        def side(beside):
            return jnp.where(beside > 0, 0.5 * (here + beside), here)

        def column(beside):
            return (0.5 * ASPECT) * (here + beside)

        marks = flat_row(clow, chigh, q)
        parts = [
            side(t_buf[q]),
            side(t_buf[q + 2]),
            side(pltpu.roll(here, 1, 1)),
            side(pltpu.roll(here, LANES - 1, 1)),
            jnp.where(level > 0, column(pltpu.roll(here, 1, 0)), 0.0),
            jnp.where(level < NZ - 1, column(pltpu.roll(here, NZ - 1, 0)), 0.0),
        ]
        total = parts[0] + parts[1] + parts[2] + parts[3] + parts[4] + parts[5]
        total = total + jnp.where(level == 0, marks, 0.0)
        inverse = jnp.where(marks > 0, 1.0 / jnp.where(marks > 0, total, 1.0), 0.0)
        for j, part in enumerate(parts):
            gs[j, q] = part * inverse
        inverse = SCALE * inverse
        inv[q] = inverse
        u_buf[q + 1] = jnp.where(level == 0, inverse * flat_row(flow, fhigh, q), 0.0)
        return 0

    lax.fori_loop(0, ROWS, faces, 0)
    close(u_buf)

    def apply(src, dst, centre, shift, first):
        def chunk(i, _):
            for k in range(CHUNK):
                q = i * CHUNK + k
                here = src[q + 1]
                new = (
                    gs[0, q] * src[q]
                    + gs[1, q] * src[q + 2]
                    + gs[2, q] * pltpu.roll(here, 1, 1)
                    + gs[3, q] * pltpu.roll(here, LANES - 1, 1)
                    + gs[4, q] * pltpu.roll(here, 1, 0)
                    + gs[5, q] * pltpu.roll(here, NZ - 1, 0)
                    + shift * (here if centre is src else centre[q + 1])
                )
                dst[q + 1] = new
            return 0

        lax.fori_loop(lax.div(first, CHUNK), ROWS // CHUNK, chunk, 0)
        close(dst)

    def pick(values, i):
        out = jnp.float32(values[0])
        for k in range(1, len(values)):
            out = jnp.where(i == k, jnp.float32(values[k]), out)
        return out

    def solve():
        apply(u_buf, t_buf, u_buf, jnp.float32(LINEAR), jnp.int32(2))

        def factor(i, _):
            apply(t_buf, u_buf, t_buf, pick(PS, i), 2 * i + 3)
            apply(u_buf, t_buf, t_buf, pick(QS, i), 2 * i + 4)
            return 0

        lax.fori_loop(0, len(PS), factor, 0)

    def columns(reduce):
        def body(i, _):
            row = reduce(t_buf[WIDE + 1 + i])
            for j in range(3):
                dlow[j, pl.ds(i, 1), :] = row[:, 128 * j : 128 * j + 128]
                dhigh[j, pl.ds(NX // 2 - 1 - i, 1), :] = row[:, 128 * j + 256 : 128 * j + 384]
            return 0

        lax.fori_loop(0, NX // 2, body, 0)
        spot = lanes_of((NX // 2, NY))
        low, high = [dlow[j] for j in range(3)], [dhigh[j] for j in range(3)]
        top = (
            jnp.where(spot < 112, turned(low[0], -16), turned(low[1], -16)),
            jnp.where(spot < 80, turned(low[1], -48), turned(low[2], -48)),
        )
        bottom = (
            jnp.where(spot < 48, turned(high[0], -80), turned(high[1], -80)),
            jnp.where(spot < 16, turned(high[1], -112), turned(high[2], -112)),
        )
        return top, bottom

    solve()
    top, bottom = columns(lambda row: jnp.sum(row, axis=0, keepdims=True))
    for k in range(2):
        depth[k, 0 : NX // 2, :] = top[k]
        depth[k, NX // 2 : NX, :] = bottom[k]
    weight = ice * obs[...]
    packed = jnp.zeros((NX, 128), F32)
    for k in range(2):
        field = weight * depth[k]
        rhs[k, own_rows, :] = field
        packed = jnp.where((lane >= 16 * k) & (lane < 16 * k + 16), turned(field, 16 * k), packed)
        at = 32 + 16 * k
        packed = jnp.where((lane >= at) & (lane < at + 16), turned(field, at - 112), packed)
    rhs_pack[...] = packed

    rhs_copies = to_neighbours(rhs, (rhs_pack, rhs_pack), (rhs_l, rhs_r), c_send, c_recv)
    start_all(rhs_copies)
    depth_out = pltpu.make_async_copy(depth, depth_ref.at[:, :, own_cols], local_sem.at[6])
    depth_out.start()
    depth_over = pltpu.make_async_remote_copy(
        depth,
        depth_ref.at[:, :, own_cols],
        swap_send.at[2],
        swap_recv.at[2],
        device_id=partner,
        device_id_type=MESH,
    )
    depth_over.start()

    arrived(rhs_copies)
    assemble(rhs, (0, 1), rhs_l, rhs_r, (32, 48), (0, 16), (flow, fhigh))

    def start_row(q, _):
        u_buf[q + 1] = inv[q] * flat_row(flow, fhigh, q)
        return 0

    lax.fori_loop(0, ROWS, start_row, 0)
    close(u_buf)
    solve()
    top, bottom = columns(lambda row: row[0:1, :])
    for half, pair in enumerate((top, bottom)):
        part = slice(half * NX // 2, (half + 1) * NX // 2)
        product = base[0, 0, part].astype(F32) * pair[0] + base[0, 1, part].astype(F32) * pair[1]
        hess[part, :] = -friction[part] * product
    hess_out = pltpu.make_async_copy(hess, hess_ref, local_sem.at[7])
    hess_out.start()

    for copies in (flat_copies, visc_copies, rhs_copies):
        sent(copies)
    depth_out.wait()
    depth_over.wait()
    hess_out.wait()


def solution(mesh):
    gx_n, gy_n = mesh.shape["gx"], mesh.shape["gy"]

    def step(viscosity, velocity, log_friction, step_dir, obs_weight, tile_mask, contact):
        any_space = pl.BlockSpec(memory_space=pl.ANY)
        vmem, dma = pltpu.VMEM, pltpu.SemaphoreType.DMA
        nd = len(DIRS)
        return pl.pallas_call(
            functools.partial(kernel, gx_n, gy_n),
            out_shape=(
                jax.ShapeDtypeStruct((2, NX, 2 * NY), F32),
                jax.ShapeDtypeStruct((NX, NY), F32),
            ),
            in_specs=[any_space] * 6 + [pl.BlockSpec(memory_space=pltpu.SMEM)],
            out_specs=(any_space, any_space),
            scratch_shapes=[
                vmem((NZ, XT, NY), BF16),
                vmem((XT, 128), BF16),
                vmem((XT, 128), BF16),
                vmem((NX, 128), BF16),
                vmem((NX, 128), BF16),
                vmem((2, 2, NX, NY), BF16),
                vmem((NX, NY), F32),
                vmem((NX, NY), F32),
                vmem((NX, NY), F32),
                vmem((NX, NY), jnp.int32),
                vmem((3, XT, NY), F32),
                vmem((NX, 128), F32),
                vmem((XT, 128), F32),
                vmem((XT, 128), F32),
                vmem((2, XT, NY), F32),
                vmem((NX, 128), F32),
                vmem((XT, 128), F32),
                vmem((XT, 128), F32),
                vmem((2, NX, NY), F32),
                vmem((NX, NY), F32),
                vmem((3, ROWS * NZ, 128), F32),
                vmem((3, ROWS * NZ, 128), F32),
                vmem((3, ROWS, 128), F32),
                vmem((3, ROWS, 128), F32),
                vmem((3, ROWS, 128), F32),
                vmem((3, ROWS, 128), F32),
                vmem((3, NX // 2, 128), F32),
                vmem((3, NX // 2, 128), F32),
                vmem((6, ROWS, NZ, LANES), F32),
                vmem((ROWS, NZ, LANES), F32),
                vmem((ROWS + 2, NZ, LANES), F32),
                vmem((ROWS + 2, NZ, LANES), F32),
                dma((8,)),
                dma((3,)),
                dma((3,)),
                dma((nd,)),
                dma((nd,)),
                dma((nd,)),
                dma((nd,)),
                dma((nd,)),
                dma((nd,)),
            ],
            compiler_params=pltpu.CompilerParams(
                collective_id=0, has_side_effects=True, vmem_limit_bytes=40 * 1024 * 1024
            ),
        )(viscosity, velocity, log_friction, step_dir, obs_weight, contact, tile_mask)

    in_specs = (
        P("gz", "gx", "gy"),
        P(None, "gz", "gx", "gy"),
        P("gx", "gy"),
        P("gx", "gy"),
        P("gx", "gy"),
        P("gx", "gy"),
        P("gx", "gy"),
    )
    out_specs = (P(None, "gx", "gy"), P("gx", ("gy", "gz")))
    return jax.shard_map(step, mesh=mesh, in_specs=in_specs, out_specs=out_specs, check_vma=False)
```

time: 880 us -> 72.4 us (0.08); the launches traced: 866 us -> 72.1 us
  starting transfers between devices: 460 us -> 0 us
  waiting for transfers between devices: 331 us -> 0 us
  Pallas kernels: 0 us -> 64.3 us
  other arithmetic: 51.4 us -> 0 us
  between operations: 17.1 us -> 0.66 us
    ppermute x187 -> x0, starting transfers between devices: 460 us -> none  [the longest x93 294 us: extended(): lax.ppermute(head, axis, [((i + 1) % count, i) for i in range(ends)])]
    ppermute x187 -> x0, waiting for transfers between devices: 307 us -> none  [the longest x93 282 us: extended(): lax.ppermute(head, axis, [((i + 1) % count, i) for i in range(ends)])]
    pallas_call x0 -> x1, Pallas kernels: none -> 64.3 us  [step(): pl.pallas_call(functools.partial(kernel, gx_n, gy_n), out_shape=(jax.Shap...]
    convert_element_type x33 -> x0, other arithmetic: 32 us -> none  [the longest x27 26 us: chebyshev(): residual = residual - operator(direction.astype(jnp.bfloat16))]
    psum x1 -> x0, waiting for transfers between devices: 24.6 us -> none  [per_device(): depth_local = lax.psum(column_sum, 'gz')]
  transfers between devices with their start and end apart: 188 -> 0, of which waited for: 126 -> 0; matrix products, arithmetic and copies ran while one was open for 0% -> 0% of each run, Pallas kernels for 0% -> 0%
where the time goes in v1:
time: 72.4 us; the launch traced here: 72.1 us
  Pallas kernels  64.3 us (89%)
  local copies, waits for them, and re-layouts  7.13 us (10%)
    pallas_call x1, Pallas kernels, step(): pl.pallas_call(functools.partial(kernel, gx_n, gy_n), out_shape=(jax.Shap...  64.3 us
    unnamed x16, local copies, waits for them, and re-layouts  7.13 us

profile of v1, /device:TPU:103, one launch (start us, length us, event | category | flops | bytes accessed | tf_op | source)
XLA Modules:
  0.0 72.1 jit_solution(7736413520536964862)
XLA Ops:
  0.6 0.0 copy-start
  0.6 0.9 %copy-done = bf16[2,4,64,256]{3,2,1,0:T(8,128)(2,1)S(1)} copy-done((bf16[2,4,64,256]{3,2,1,0:T(8,128)(2,1)S(1)}, bf16[2,4,64,256]{3,2,1,0:T(8,128)(2,1)}, u32[]{:S(2)}) %copy-start) | copy-done | bytes 262168
  1.6 0.0 copy-start.1
  1.6 0.9 %copy-done.1 = bf16[4,64,256]{2,1,0:T(8,128)(2,1)S(1)} copy-done((bf16[4,64,256]{2,1,0:T(8,128)(2,1)S(1)}, bf16[4,64,256]{2,1,0:T(8,128)(2,1)}, u32[]{:S(2)}) %copy-start.1) | copy-done | bytes 131096
  2.5 0.0 copy-start.2
  2.5 0.8 %copy-done.2 = f32[64,256]{1,0:T(8,128)S(1)} copy-done((f32[64,256]{1,0:T(8,128)S(1)}, f32[64,256]{1,0:T(8,128)}, u32[]{:S(2)}) %copy-start.2) | copy-done | bytes 65560
  3.3 0.0 copy-start.3
  3.3 0.8 %copy-done.3 = f32[64,256]{1,0:T(8,128)S(1)} copy-done((f32[64,256]{1,0:T(8,128)S(1)}, f32[64,256]{1,0:T(8,128)}, u32[]{:S(2)}) %copy-start.3) | copy-done | bytes 65560
  4.2 0.0 copy-start.4
  4.2 0.8 %copy-done.4 = f32[64,256]{1,0:T(8,128)S(1)} copy-done((f32[64,256]{1,0:T(8,128)S(1)}, f32[64,256]{1,0:T(8,128)}, u32[]{:S(2)}) %copy-start.4) | copy-done | bytes 65560
  5.0 0.0 copy-start.5
  5.0 0.8 %copy-done.5 = s32[64,256]{1,0:T(8,128)S(1)} copy-done((s32[64,256]{1,0:T(8,128)S(1)}, s32[64,256]{1,0:T(8,128)}, u32[]{:S(2)}) %copy-start.5) | copy-done | bytes 65560
  5.8 0.0 copy-start.6
  5.8 0.7 copy-done.6
  6.5 64.3 %shard_map.86 = (f32[2,64,256]{2,1,0:T(8,128)S(1)}, f32[64,128]{1,0:T(8,128)S(1)}) custom-call(bf16[4,64,256]{2,1,0:T(8,128)(2,1)S(1)} %copy-done.1, bf16[2,4,64,256]{3,2,1,0:T(8,128)(2,1)S(1)} %copy-done, f32[64,256]{1,0:T(8,128)S(1)} %copy-done.2, f32[64,256]{1,0:T(8,128)S(1)} %copy-done.3, f32[64,256]{1,0:T(8,128)S(1)} %copy-done.4, ...), custom_call_target="tpu_custom_call" | custom-call | tf_op jit(solution)/shard_map/pallas_call | solution.py:520
  70.8 0.7 copy.11
  71.4 0.6 copy.12
Async XLA Ops:
  0.6 1.0 %copy-start = (bf16[2,4,64,256]{3,2,1,0:T(8,128)(2,1)S(1)}, bf16[2,4,64,256]{3,2,1,0:T(8,128)(2,1)}, u32[]{:S(2)}) copy-start(bf16[2,4,64,256]{3,2,1,0:T(8,128)(2,1)} %vel_ref.1) | copy-start | bytes 786436
  1.6 0.9 %copy-start.1 = (bf16[4,64,256]{2,1,0:T(8,128)(2,1)S(1)}, bf16[4,64,256]{2,1,0:T(8,128)(2,1)}, u32[]{:S(2)}) copy-start(bf16[4,64,256]{2,1,0:T(8,128)(2,1)} %visc_ref.1) | copy-start | bytes 393220
  2.5 0.8 %copy-start.2 = (f32[64,256]{1,0:T(8,128)S(1)}, f32[64,256]{1,0:T(8,128)}, u32[]{:S(2)}) copy-start(f32[64,256]{1,0:T(8,128)} %logf_ref.1) | copy-start | bytes 196612
  3.3 0.8 %copy-start.3 = (f32[64,256]{1,0:T(8,128)S(1)}, f32[64,256]{1,0:T(8,128)}, u32[]{:S(2)}) copy-start(f32[64,256]{1,0:T(8,128)} %step_ref.1) | copy-start | bytes 196612
  4.2 0.8 %copy-start.4 = (f32[64,256]{1,0:T(8,128)S(1)}, f32[64,256]{1,0:T(8,128)}, u32[]{:S(2)}) copy-start(f32[64,256]{1,0:T(8,128)} %obs_ref.1) | copy-start | bytes 196612
  5.0 0.8 %copy-start.5 = (s32[64,256]{1,0:T(8,128)S(1)}, s32[64,256]{1,0:T(8,128)}, u32[]{:S(2)}) copy-start(s32[64,256]{1,0:T(8,128)} %contact_ref.1) | copy-start | bytes 196612
  5.8 0.7 copy-start.6

commit v2 on v1

--- a/solution.py
+++ b/solution.py
@@ -36,9 +36,9 @@
 NX, NY, NZ = 64, 128, 8
 ROWS = NX // 2 + WIDE
 XT = NX + 2 * WIDE
-LANES = 4 * (NY + 2 * WIDE)
-TILES = LANES // 128
-CHUNK = 4
+FINE = 5
+BLOCKS = (NY + 2 * WIDE) // FINE
+CHUNK = 8
 DIRS = [(dx, dy) for dx in (-1, 0, 1) for dy in (-1, 0, 1) if (dx, dy) != (0, 0)]
 
 
@@ -51,37 +51,51 @@
     return value if by == 0 else pltpu.roll(value, by, value.ndim - 1)
 
 
-def triple_low(own, left, right):
-    lane = lanes_of(own[0].shape)
-
-    def put(piece, to):
-        return turned(piece[0], to - piece[1])
-
-    a, b = turned(own[0], 16), turned(own[1], 48)
-    t0 = jnp.where(lane < 16, put(left[0], 0), a)
-    t1 = jnp.where(lane < 16, a, jnp.where(lane < 32, put(right[0], 16), jnp.where(lane < 48, put(left[1], 32), b)))
-    t2 = jnp.where(lane < 48, b, put(right[1], 48))
-    return t0, t1, t2
-
-
-def triple_high(own, left, right):
-    lane = lanes_of(own[0].shape)
-
-    def put(piece, to):
-        return turned(piece[0], to - piece[1])
-
-    a, b = turned(own[0], 80), turned(own[1], 112)
-    t2 = jnp.where(lane < 80, put(left[0], 64), a)
-    t3 = jnp.where(
-        lane < 80, a, jnp.where(lane < 96, put(right[0], 80), jnp.where(lane < 112, put(left[1], 96), b))
-    )
-    t4 = jnp.where(lane < 112, b, put(right[1], 112))
-    return t2, t3, t4
-
-
-def joined_tiles(low, high):
-    middle = jnp.where(lanes_of(low[2].shape) < 64, low[2], high[0])
-    return jnp.concatenate([low[0], low[1], middle, high[1], high[2]], axis=-1)
+def chooser(rows, fine, spot):
+    k = lax.broadcasted_iota(jnp.int32, (rows, 128), 0)
+    n = lanes_of((rows, 128))
+    y = FINE * (n % BLOCKS) + fine
+    return (k == spot(n // 64, (n // BLOCKS) % 2, y)).astype(F32).astype(BF16)
+
+
+def spot_single(half, component, y):
+    edge = jnp.where(y < WIDE, 128 + 80 + y, 128 + 32 + y - WIDE - NY)
+    k = 256 * half + jnp.where((y >= WIDE) & (y < WIDE + NY), y - WIDE, edge)
+    return jnp.where((y >= 0) & (y < NY + 2 * WIDE), k, -1)
+
+
+def spot_pair(half, component, y):
+    edge = 256 + 16 * component + jnp.where(y < WIDE, 48 + y, y - WIDE - NY)
+    return 384 * half + jnp.where((y >= WIDE) & (y < WIDE + NY), 128 * component + y - WIDE, edge)
+
+
+def returner(half, component):
+    k = lax.broadcasted_iota(jnp.int32, (FINE * 128, NY), 0)
+    y = lanes_of((FINE * 128, NY)) + WIDE
+    source = (y % FINE) * 128 + 64 * half + BLOCKS * component + y // FINE
+    return (k == source).astype(F32).astype(BF16)
+
+
+def mirror(n):
+    k = lax.broadcasted_iota(jnp.int32, (n, n), 0)
+    return (k + lanes_of((n, n)) == n - 1).astype(F32).astype(BF16)
+
+
+def thirds(value):
+    high = value.astype(BF16)
+    rest = value - high.astype(F32)
+    middle = rest.astype(BF16)
+    return high, middle, (rest - middle.astype(F32)).astype(BF16)
+
+
+def dot(a, b):
+    return jnp.dot(a, b, preferred_element_type=F32)
+
+
+def exact_dot(value, matrix):
+    n = value.shape[0]
+    out = dot(jnp.concatenate(thirds(value), axis=0), matrix)
+    return out[:n] + out[n : 2 * n] + out[2 * n :]
 
 
 def kernel(
@@ -116,16 +130,18 @@
     rhs_r,
     depth,
     hess,
-    vlow,
-    vhigh,
-    flow,
-    fhigh,
-    clow,
-    chigh,
+    left,
+    e_buf,
+    spread_f,
+    spread_c,
     dlow,
     dhigh,
+    single,
+    pair,
+    back,
     gs,
     inv,
+    ext,
     u_buf,
     t_buf,
     local_sem,
@@ -197,6 +213,17 @@
             def _():
                 for end in ends:
                     end[first : first + count, :] = jnp.zeros((count, 128), end.dtype)
+
+    for fine in range(FINE):
+        lot = slice(128 * fine, 128 * fine + 128)
+        single[:, lot] = chooser(512, fine, spot_single)
+        pair[:, lot] = chooser(768, fine, spot_pair)
+    single[:, 128 * FINE : 128 * (FINE + 1)] = chooser(512, -1, spot_single)
+    single[:, 128 * (FINE + 1) : 128 * (FINE + 2)] = chooser(512, FINE, spot_single)
+    for half in range(2):
+        for component in range(2):
+            at = 128 * (2 * half + component)
+            back[:, at : at + 128] = returner(half, component)
 
     pl.semaphore_wait(barrier, met)
 
@@ -313,111 +340,154 @@
     arrived(flat_copies)
     arrived(visc_copies)
 
-    def spread_rows(i, _):
-        for half, (place, out) in enumerate(((triple_low, vlow), (triple_high, vhigh))):
-            rows = pl.ds(pl.multiple_of(half * ROWS + i * 16, 16), 16)
-            ends_l, ends_r = edge_l[rows, :].astype(F32), edge_r[rows, :].astype(F32)
-            for layer in range(NZ):
-                own = visc[layer, rows, :].astype(F32)
-                lefts, rights = (ends_l, 16 * layer), (ends_r, 16 * layer)
-                for j, tile in enumerate(place((own, own), (lefts, lefts), (rights, rights))):
-                    out[j, pl.ds(i * 16 * NZ + layer, 16, stride=NZ), :] = tile
+    low_rows, high_rows = slice(0, ROWS), slice(ROWS, XT)
+    flipped = mirror(ROWS)
+
+    spot = lanes_of((ROWS, 128))
+    turned_rows = []
+    for half, rows in enumerate((low_rows, high_rows)):
+        ends_l, ends_r = edge_l[rows, :].astype(F32), edge_r[rows, :].astype(F32)
+        for layer in range(NZ):
+            edge = jnp.where(spot < 64, turned(ends_r, 32 - 16 * layer), turned(ends_l, 80 - 16 * layer))
+            edge = edge.astype(BF16)
+            own = visc[layer, rows, :]
+            if half == 1:
+                both = dot(flipped, jnp.concatenate([own, edge], axis=1)).astype(BF16)
+                own, edge = both[:, :128], both[:, 128:]
+            here = slice(ROWS * layer, ROWS * layer + ROWS)
+            left[here, 256 * half : 256 * half + 128] = own
+            left[here, 256 * half + 128 : 256 * half + 256] = edge
+
+    tiles = FINE + 2
+    for fine in range(tiles):
+        placed = 0.5 * dot(left[...], single[:, 128 * fine : 128 * fine + 128])
+        for layer in range(NZ):
+            e_buf[pl.ds(tiles * NZ + fine * NZ + layer, ROWS, stride=tiles * NZ), :] = placed[
+                ROWS * layer : ROWS * layer + ROWS
+            ]
+    e_buf[0 : tiles * NZ, :] = jnp.zeros((tiles * NZ, 128), F32)
+
+    def e_tile(row, fine):
+        return pl.ds(pl.multiple_of((row * tiles + fine) * NZ, NZ), NZ)
+
+    for fine in range(FINE):
+        e_buf[e_tile(ROWS + 1, fine), :] = pltpu.roll(e_buf[e_tile(ROWS, fine), :], 64, 1)
+
+    def both_halves(pieces):
+        low, high = pieces(low_rows), thirds(pieces(high_rows))
+        width = low.shape[1]
+        high = dot(flipped, jnp.concatenate(high, axis=1))
+        return jnp.concatenate([low, high[:, :width] + high[:, width : 2 * width] + high[:, 2 * width :]], axis=1)
+
+    def edges(rows, ends_l, ends_r):
+        return jnp.where(spot < 48, ends_r[rows, :], ends_l[rows, :])
+
+    def put(out, value):
+        for fine in range(FINE):
+            out[fine] = value[:, 128 * fine : 128 * fine + 128]
+
+    marks_placed = exact_dot(
+        both_halves(lambda rows: jnp.concatenate([flat[2, rows, :], edges(rows, flat_l, flat_r)], axis=1)),
+        single[:, : 128 * FINE],
+    )
+    put(spread_c, marks_placed)
+
+    def spread_pair(own, ends_l, ends_r):
+        placed = exact_dot(
+            both_halves(
+                lambda rows: jnp.concatenate([own[0, rows, :], own[1, rows, :], edges(rows, ends_l, ends_r)], axis=1)
+            ),
+            pair[...],
+        )
+        put(spread_f, placed)
+
+    spread_pair(flat, flat_l, flat_r)
+
+    level = lax.broadcasted_iota(jnp.int32, (NZ, 128), 0)
+
+    def flat_tile(field, q, fine):
+        return jnp.broadcast_to(field[fine, pl.ds(q, 1), :], (NZ, 128))
+
+    def faces(q, _):
+        for fine in range(FINE):
+            here = e_buf[e_tile(q + 1, fine), :]
+
+            def side(beside):
+                return here + jnp.where(beside > 0, beside, here)
+
+            def column(beside):
+                return ASPECT * (here + beside)
+
+            marks = flat_tile(spread_c, q, fine)
+            parts = [
+                side(e_buf[e_tile(q, fine), :]),
+                side(e_buf[e_tile(q + 2, fine), :]),
+                side(e_buf[e_tile(q + 1, fine - 1 if fine else FINE), :]),
+                side(e_buf[e_tile(q + 1, fine + 1 if fine < FINE - 1 else FINE + 1), :]),
+                jnp.where(level > 0, column(pltpu.roll(here, 1, 0)), 0.0),
+                jnp.where(level < NZ - 1, column(pltpu.roll(here, NZ - 1, 0)), 0.0),
+            ]
+            total = parts[0] + parts[1] + parts[2] + parts[3] + parts[4] + parts[5]
+            total = total + jnp.where(level == 0, marks, 0.0)
+            inverse = jnp.where(marks > 0, 1.0 / jnp.where(marks > 0, total, 1.0), 0.0)
+            for j, part in enumerate(parts):
+                gs[q, fine, j] = part * inverse
+            inverse = SCALE * inverse
+            inv[q, fine] = inverse
+            u_buf[q + 1, fine] = jnp.where(level == 0, inverse * flat_tile(spread_f, q, fine), 0.0)
         return 0
 
-    lax.fori_loop(0, ROWS // 16, spread_rows, 0)
-
-    def eight(i):
-        return pl.ds(pl.multiple_of(i * NZ, NZ), NZ)
-
-    t_buf[0] = jnp.zeros((NZ, LANES), F32)
-    u_buf[0] = jnp.zeros((NZ, LANES), F32)
-
-    def join_row(q, _):
-        low = [vlow[j, eight(q), :] for j in range(3)]
-        high = [vhigh[j, eight(ROWS - 1 - q), :] for j in range(3)]
-        t_buf[q + 1] = joined_tiles(low, high)
-        return 0
-
-    lax.fori_loop(0, ROWS, join_row, 0)
-
-    def close(buf):
-        buf[ROWS + 1] = pltpu.roll(buf[ROWS], LANES // 2, 1)
-
-    close(t_buf)
-
-    def assemble(own, which, ends_l, ends_r, spots_l, spots_r, outs):
-        def body(i, _):
-            for half, (place, out) in enumerate(((triple_low, outs[0]), (triple_high, outs[1]))):
-                rows = pl.ds(pl.multiple_of(half * ROWS + i * 8, 8), 8)
-                l, r = ends_l[rows, :], ends_r[rows, :]
-                pieces = [own[k, rows, :] for k in which]
-                tiles = place(pieces, [(l, s) for s in spots_l], [(r, s) for s in spots_r])
-                for j, tile in enumerate(tiles):
-                    out[j, pl.ds(pl.multiple_of(i * 8, 8), 8), :] = tile
+    lax.fori_loop(0, ROWS, faces, 0)
+    for fine in range(FINE):
+        u_buf[0, fine] = jnp.zeros((NZ, 128), F32)
+        t_buf[0, fine] = jnp.zeros((NZ, 128), F32)
+        t_buf[ROWS, fine] = jnp.zeros((NZ, 128), F32)
+
+    def begin(buf):
+        for fine in range(FINE):
+            buf[ROWS + 1, fine] = pltpu.roll(buf[ROWS, fine], 64, 1)
+        for k in range(CHUNK):
+            row = ROWS - CHUNK + k + 1
+            ext[k, 0] = pltpu.roll(buf[row, FINE - 1], 1, 1)
+            ext[k, 1] = pltpu.roll(buf[row, 0], 127, 1)
+
+    def apply(src, dst, centre, shift, first):
+        n = lax.div(ROWS - first + CHUNK - 1, CHUNK)
+
+        def chunk(i, _):
+            q0 = ROWS - CHUNK * (i + 1)
+            more = i + 1 < n
+            ahead = jnp.maximum(q0 - CHUNK, 0)
+            across = [(ext[k, 0], ext[k, 1]) for k in range(CHUNK)]
+            later = []
+            for k in range(CHUNK):
+                row, again = ahead + k + 1, ROWS - CHUNK + k + 1
+                up = jnp.where(more, src[row, FINE - 1], dst[again, FINE - 1])
+                down = jnp.where(more, src[row, 0], dst[again, 0])
+                later.append((pltpu.roll(up, 1, 1), pltpu.roll(down, 127, 1)))
+            closing = [pltpu.roll(dst[ROWS, fine], 64, 1) for fine in range(FINE)]
+            for k in range(CHUNK):
+                q = q0 + k
+                here = [src[q + 1, fine] for fine in range(FINE)]
+                for fine in range(FINE):
+                    before = here[fine - 1] if fine else across[k][0]
+                    after = here[fine + 1] if fine < FINE - 1 else across[k][1]
+                    new = (
+                        (gs[q, fine, 0] * src[q, fine] + gs[q, fine, 1] * src[q + 2, fine])
+                        + (gs[q, fine, 2] * before + gs[q, fine, 3] * after)
+                        + (
+                            gs[q, fine, 4] * pltpu.roll(here[fine], 1, 0)
+                            + gs[q, fine, 5] * pltpu.roll(here[fine], NZ - 1, 0)
+                        )
+                    )
+                    dst[q + 1, fine] = new + shift * (here[fine] if centre is src else centre[q + 1, fine])
+            for k in range(CHUNK):
+                ext[k, 0], ext[k, 1] = later[k]
+            for fine in range(FINE):
+                dst[ROWS + 1, fine] = closing[fine]
             return 0
 
-        lax.fori_loop(0, ROWS // 8, body, 0)
-
-    def flat_row(low, high, q):
-        one = [low[j, pl.ds(q, 1), :] for j in range(3)]
-        two = [high[j, pl.ds(ROWS - 1 - q, 1), :] for j in range(3)]
-        return jnp.broadcast_to(joined_tiles(one, two), (NZ, LANES))
-
-    assemble(flat, (2, 2), flat_l, flat_r, (80, 80), (32, 32), (clow, chigh))
-    assemble(flat, (0, 1), flat_l, flat_r, (48, 64), (0, 16), (flow, fhigh))
-
-    level = lax.broadcasted_iota(jnp.int32, (NZ, LANES), 0)
-
-    def faces(q, _):
-        here = t_buf[q + 1]
-
-        def side(beside):
-            return jnp.where(beside > 0, 0.5 * (here + beside), here)
-
-        def column(beside):
-            return (0.5 * ASPECT) * (here + beside)
-
-        marks = flat_row(clow, chigh, q)
-        parts = [
-            side(t_buf[q]),
-            side(t_buf[q + 2]),
-            side(pltpu.roll(here, 1, 1)),
-            side(pltpu.roll(here, LANES - 1, 1)),
-            jnp.where(level > 0, column(pltpu.roll(here, 1, 0)), 0.0),
-            jnp.where(level < NZ - 1, column(pltpu.roll(here, NZ - 1, 0)), 0.0),
-        ]
-        total = parts[0] + parts[1] + parts[2] + parts[3] + parts[4] + parts[5]
-        total = total + jnp.where(level == 0, marks, 0.0)
-        inverse = jnp.where(marks > 0, 1.0 / jnp.where(marks > 0, total, 1.0), 0.0)
-        for j, part in enumerate(parts):
-            gs[j, q] = part * inverse
-        inverse = SCALE * inverse
-        inv[q] = inverse
-        u_buf[q + 1] = jnp.where(level == 0, inverse * flat_row(flow, fhigh, q), 0.0)
-        return 0
-
-    lax.fori_loop(0, ROWS, faces, 0)
-    close(u_buf)
-
-    def apply(src, dst, centre, shift, first):
-        def chunk(i, _):
-            for k in range(CHUNK):
-                q = i * CHUNK + k
-                here = src[q + 1]
-                new = (
-                    gs[0, q] * src[q]
-                    + gs[1, q] * src[q + 2]
-                    + gs[2, q] * pltpu.roll(here, 1, 1)
-                    + gs[3, q] * pltpu.roll(here, LANES - 1, 1)
-                    + gs[4, q] * pltpu.roll(here, 1, 0)
-                    + gs[5, q] * pltpu.roll(here, NZ - 1, 0)
-                    + shift * (here if centre is src else centre[q + 1])
-                )
-                dst[q + 1] = new
-            return 0
-
-        lax.fori_loop(lax.div(first, CHUNK), ROWS // CHUNK, chunk, 0)
-        close(dst)
+        lax.fori_loop(0, n, chunk, 0)
 
     def pick(values, i):
         out = jnp.float32(values[0])
@@ -426,6 +496,7 @@
         return out
 
     def solve():
+        begin(u_buf)
         apply(u_buf, t_buf, u_buf, jnp.float32(LINEAR), jnp.int32(2))
 
         def factor(i, _):
@@ -437,24 +508,18 @@
 
     def columns(reduce):
         def body(i, _):
-            row = reduce(t_buf[WIDE + 1 + i])
-            for j in range(3):
-                dlow[j, pl.ds(i, 1), :] = row[:, 128 * j : 128 * j + 128]
-                dhigh[j, pl.ds(NX // 2 - 1 - i, 1), :] = row[:, 128 * j + 256 : 128 * j + 384]
+            for k in range(4):
+                q = 4 * i + k
+                for fine in range(FINE):
+                    row = reduce(t_buf[WIDE + 1 + q, fine])
+                    dlow[fine, pl.ds(q, 1), :] = row
+                    dhigh[fine, pl.ds(NX // 2 - 1 - q, 1), :] = row
             return 0
 
-        lax.fori_loop(0, NX // 2, body, 0)
-        spot = lanes_of((NX // 2, NY))
-        low, high = [dlow[j] for j in range(3)], [dhigh[j] for j in range(3)]
-        top = (
-            jnp.where(spot < 112, turned(low[0], -16), turned(low[1], -16)),
-            jnp.where(spot < 80, turned(low[1], -48), turned(low[2], -48)),
-        )
-        bottom = (
-            jnp.where(spot < 48, turned(high[0], -80), turned(high[1], -80)),
-            jnp.where(spot < 16, turned(high[1], -112), turned(high[2], -112)),
-        )
-        return top, bottom
+        lax.fori_loop(0, NX // 8, body, 0)
+        low = exact_dot(jnp.concatenate([dlow[fine] for fine in range(FINE)], axis=1), back[:, :256])
+        high = exact_dot(jnp.concatenate([dhigh[fine] for fine in range(FINE)], axis=1), back[:, 256:])
+        return (low[:, :128], low[:, 128:]), (high[:, :128], high[:, 128:])
 
     solve()
     top, bottom = columns(lambda row: jnp.sum(row, axis=0, keepdims=True))
@@ -467,7 +532,7 @@
         field = weight * depth[k]
         rhs[k, own_rows, :] = field
         packed = jnp.where((lane >= 16 * k) & (lane < 16 * k + 16), turned(field, 16 * k), packed)
-        at = 32 + 16 * k
+        at = 48 + 16 * k
         packed = jnp.where((lane >= at) & (lane < at + 16), turned(field, at - 112), packed)
     rhs_pack[...] = packed
 
@@ -486,14 +551,16 @@
     depth_over.start()
 
     arrived(rhs_copies)
-    assemble(rhs, (0, 1), rhs_l, rhs_r, (32, 48), (0, 16), (flow, fhigh))
-
-    def start_row(q, _):
-        u_buf[q + 1] = inv[q] * flat_row(flow, fhigh, q)
+    spread_pair(rhs, rhs_l, rhs_r)
+
+    def start_rows(i, _):
+        for k in range(4):
+            q = 4 * i + k
+            for fine in range(FINE):
+                u_buf[q + 1, fine] = inv[q, fine] * flat_tile(spread_f, q, fine)
         return 0
 
-    lax.fori_loop(0, ROWS, start_row, 0)
-    close(u_buf)
+    lax.fori_loop(0, ROWS // 4, start_rows, 0)
     solve()
     top, bottom = columns(lambda row: row[0:1, :])
     for half, pair in enumerate((top, bottom)):
@@ -546,18 +613,20 @@
                 vmem((XT, 128), F32),
                 vmem((2, NX, NY), F32),
                 vmem((NX, NY), F32),
-                vmem((3, ROWS * NZ, 128), F32),
-                vmem((3, ROWS * NZ, 128), F32),
-                vmem((3, ROWS, 128), F32),
-                vmem((3, ROWS, 128), F32),
-                vmem((3, ROWS, 128), F32),
-                vmem((3, ROWS, 128), F32),
-                vmem((3, NX // 2, 128), F32),
-                vmem((3, NX // 2, 128), F32),
-                vmem((6, ROWS, NZ, LANES), F32),
-                vmem((ROWS, NZ, LANES), F32),
-                vmem((ROWS + 2, NZ, LANES), F32),
-                vmem((ROWS + 2, NZ, LANES), F32),
+                vmem((ROWS * NZ, 512), BF16),
+                vmem(((ROWS + 2) * (FINE + 2) * NZ, 128), F32),
+                vmem((FINE, ROWS, 128), F32),
+                vmem((FINE, ROWS, 128), F32),
+                vmem((FINE, NX // 2, 128), F32),
+                vmem((FINE, NX // 2, 128), F32),
+                vmem((512, (FINE + 2) * 128), BF16),
+                vmem((768, FINE * 128), BF16),
+                vmem((FINE * 128, 512), BF16),
+                vmem((ROWS, FINE, 6, NZ, 128), F32),
+                vmem((ROWS, FINE, NZ, 128), F32),
+                vmem((CHUNK, 2, NZ, 128), F32),
+                vmem((ROWS + 2, FINE, NZ, 128), F32),
+                vmem((ROWS + 2, FINE, NZ, 128), F32),
                 dma((8,)),
                 dma((3,)),
                 dma((3,)),
@@ -569,7 +638,7 @@
                 dma((nd,)),
             ],
             compiler_params=pltpu.CompilerParams(
-                collective_id=0, has_side_effects=True, vmem_limit_bytes=40 * 1024 * 1024
+                collective_id=0, has_side_effects=True, vmem_limit_bytes=67043328
             ),
         )(viscosity, velocity, log_friction, step_dir, obs_weight, contact, tile_mask)
 

time: 72.4 us -> 43.5 us (0.60)
  Pallas kernels: 64.3 us -> 40.5 us
  local copies, waits for them, and re-layouts: 7.13 us -> 2.19 us
    pallas_call x1, Pallas kernels: 64.3 us -> 40.5 us  [step(): pl.pallas_call(functools.partial(kernel, gx_n, gy_n), out_shape=(jax.Shap...]
    unnamed x16 -> x4, local copies, waits for them, and re-layouts: 7.13 us -> 2.19 us
where the time goes in v2:
time: 43.5 us; the launch traced here: 43.3 us
  Pallas kernels  40.5 us (93%)
  local copies, waits for them, and re-layouts  2.19 us (5%)
  between operations  0.65 us (1%)
    pallas_call x1, Pallas kernels, step(): pl.pallas_call(functools.partial(kernel, gx_n, gy_n), out_shape=(jax.Shap...  40.5 us
    unnamed x4, local copies, waits for them, and re-layouts  2.19 us

profile of v2, /device:TPU:103, one launch (start us, length us, event | category | flops | bytes accessed | tf_op | source)
XLA Modules:
  0.0 43.3 jit_solution(12475241074837152775)
XLA Ops:
  0.6 40.5 %shard_map.86 = (f32[2,64,256]{2,1,0:T(8,128)}, f32[64,128]{1,0:T(8,128)}) custom-call(bf16[4,64,256]{2,1,0:T(8,128)(2,1)} %visc_ref.1, bf16[2,4,64,256]{3,2,1,0:T(8,128)(2,1)} %vel_ref.1, f32[64,256]{1,0:T(8,128)} %logf_ref.1, f32[64,256]{1,0:T(8,128)} %step_ref.1, f32[64,256]{1,0:T(8,128)} %obs_ref.1, s32[64,256]{1,0:T(8,128)} %contact_ref.1, s32[1,4]{1,0:T(1,128)} %tile_ref.1), custom_call_target="tpu_custom_call" | custom-call | tf_op jit(solution)/shard_map/pallas_call | solution.py:587
  41.1 0.0 copy-start
  41.1 1.6 %copy.11 = f32[2,64,256]{2,1,0:T(8,128)} copy(f32[2,64,256]{2,1,0:T(8,128)} %get-tuple-element.4) | data formatting | bytes 262144
  42.7 0.0 copy-done
  42.7 0.6 %copy.12 = f32[64,128]{1,0:T(8,128)} copy(f32[64,128]{1,0:T(8,128)S(1)} %copy-done) | data formatting | bytes 65536
Async XLA Ops:
  41.1 1.6 %copy-start = (f32[64,128]{1,0:T(8,128)S(1)}, f32[64,128]{1,0:T(8,128)}, u32[]{:S(2)}) copy-start(f32[64,128]{1,0:T(8,128)} %get-tuple-element.5) | copy-start | bytes 98308

commit v3 on v2

v3 whole, which is shorter than its diff:
```python
import functools
import math

import jax
import jax.numpy as jnp
from jax import lax
from jax.experimental import pallas as pl
from jax.experimental.pallas import tpu as pltpu
from jax.sharding import PartitionSpec as P

MESH = pl.DeviceIdType.MESH
F32 = jnp.float32
BF16 = jnp.bfloat16

SWEEP = 8
ASPECT = 16.0
LOWER = 0.1
UPPER = 2.0
CENTRE = (UPPER + LOWER) / 2.0
HALF = (UPPER - LOWER) / 2.0
SIGMA = CENTRE / HALF

DELTA = CENTRE - 1.0
LINEAR = DELTA + CENTRE
ORDER = (3, 6, 1, 4, 5, 2, 7)
ANGLES = [math.pi * j / SWEEP for j in ORDER]
PS = [2.0 * DELTA - 2.0 * CENTRE * math.cos(t) for t in ANGLES]
QS = [
    DELTA * DELTA - 2.0 * CENTRE * DELTA * math.cos(t) + CENTRE * CENTRE - (HALF * math.sin(t)) ** 2
    for t in ANGLES
]
TOP = math.cosh(SWEEP * math.acosh(SIGMA))
SCALE = 2.0 ** (2 * SWEEP - 2) / (TOP * TOP) / HALF ** (2 * SWEEP)

WIDE = 16
NX, NY, NZ = 64, 128, 8
XT, YT = NX + 2 * WIDE, NY + 2 * WIDE
LOTS = 4
ROWS = XT // LOTS
BLOCKS = 128 // LOTS
FINE = YT // BLOCKS
DIRS = [(dx, dy) for dx in (-1, 0, 1) for dy in (-1, 0, 1) if (dx, dy) != (0, 0)]
R_AT, L_AT = 32, 80
ROW_ORDER = [ROWS - 1, *range(8), *range(ROWS - 2, 15, -1), *range(8, 16)]
LATE = range(12, 16)


def lanes_of(shape):
    return lax.broadcasted_iota(jnp.int32, shape, len(shape) - 1)


def turned(value, by):
    by %= 128
    return value if by == 0 else pltpu.roll(value, by, value.ndim - 1)


def one_in(rows, target):
    return (lax.broadcasted_iota(jnp.int32, (rows, 128), 0) == target).astype(F32).astype(BF16)


def chooser(fine):
    n = lanes_of((1, 128))
    y = FINE * (n % BLOCKS) + fine
    edge = jnp.where(y < WIDE, 128 + L_AT + y, 128 + R_AT + y - WIDE - NY)
    k = 256 * (n // BLOCKS) + jnp.where((y >= WIDE) & (y < WIDE + NY), y - WIDE, edge)
    return one_in(256 * LOTS, jnp.where((y >= 0) & (y < YT), k, -1))


def returner(lot):
    y = lanes_of((1, 128)) + WIDE
    return one_in(FINE * 128, (y % FINE) * 128 + BLOCKS * lot + y // FINE)


def thirds(value):
    high = value.astype(BF16)
    rest = value - high.astype(F32)
    middle = rest.astype(BF16)
    return high, middle, (rest - middle.astype(F32)).astype(BF16)


def dot(a, b):
    return jnp.dot(a, b, preferred_element_type=F32)


def exact_dot(value, matrix):
    n = value.shape[0]
    out = dot(jnp.concatenate(thirds(value), axis=0), matrix)
    return out[:n] + out[n : 2 * n] + out[2 * n :]


def kernel(
    gx_n,
    gy_n,
    visc_ref,
    vel_ref,
    logf_ref,
    step_ref,
    obs_ref,
    contact_ref,
    tile_ref,
    depth_ref,
    hess_ref,
    visc,
    edge_l,
    edge_r,
    pack_l,
    pack_r,
    base,
    logf,
    step,
    obs,
    contact,
    flat,
    flat_pack,
    flat_l,
    flat_r,
    rhs,
    rhs_pack,
    rhs_l,
    rhs_r,
    depth,
    hess,
    mult,
    left,
    e_buf,
    spread,
    sums,
    place,
    back,
    gs,
    inv,
    u_ext,
    t_ext,
    u_buf,
    t_buf,
    classes,
    local_sem,
    swap_send,
    swap_recv,
    a_send,
    a_recv,
    b_send,
    b_recv,
    c_send,
    c_recv,
):
    gx, gy, gz = lax.axis_index("gx"), lax.axis_index("gy"), lax.axis_index("gz")
    yb = 2 * gy + gz
    y_n = 2 * gy_n

    def there(dx, dy):
        nx, ny = gx + dx, yb + dy
        return (nx >= 0) & (nx < gx_n) & (ny >= 0) & (ny < y_n)

    def device(dx, dy):
        ny = yb + dy
        return (gx + dx, lax.div(ny, 2), lax.rem(ny, 2))

    own_cols = pl.ds(pl.multiple_of(gz * NY, NY), NY)
    other_cols = pl.ds(pl.multiple_of((1 - gz) * NY, NY), NY)
    own_rows = pl.ds(WIDE, NX)
    layers = visc_ref.shape[0]
    mine = pl.ds(gz * layers, layers)
    partner = (gx, gy, 1 - gz)

    local = [
        pltpu.make_async_copy(visc_ref.at[:, :, own_cols], visc.at[mine, own_rows], local_sem.at[0]),
        pltpu.make_async_copy(vel_ref.at[:, 0, :, own_cols], base.at[gz], local_sem.at[1]),
        pltpu.make_async_copy(logf_ref.at[:, own_cols], logf, local_sem.at[2]),
        pltpu.make_async_copy(step_ref.at[:, own_cols], step, local_sem.at[3]),
        pltpu.make_async_copy(contact_ref.at[:, own_cols], contact, local_sem.at[4]),
        pltpu.make_async_copy(obs_ref.at[:, own_cols], obs, local_sem.at[5]),
        pltpu.make_async_copy(tile_ref, classes, local_sem.at[6]),
    ]
    for copy in local:
        copy.start()

    barrier = pltpu.get_barrier_semaphore()
    met = 0
    for d in DIRS:
        here = there(*d)
        met = met + here.astype(jnp.int32)

        @pl.when(here)
        def _():
            pl.semaphore_signal(barrier, inc=1, device_id=device(*d), device_id_type=MESH)

    @pl.when(gx == 0)
    def _():
        visc[:, 0:WIDE, :] = jnp.zeros((NZ, WIDE, NY), BF16)
        flat[:, 0:WIDE, :] = jnp.zeros((3, WIDE, NY), F32)
        rhs[:, 0:WIDE, :] = jnp.zeros((2, WIDE, NY), F32)

    @pl.when(gx == gx_n - 1)
    def _():
        visc[:, XT - WIDE : XT, :] = jnp.zeros((NZ, WIDE, NY), BF16)
        flat[:, XT - WIDE : XT, :] = jnp.zeros((3, WIDE, NY), F32)
        rhs[:, XT - WIDE : XT, :] = jnp.zeros((2, WIDE, NY), F32)

    for dy, ends in ((-1, (edge_l, flat_l, rhs_l)), (1, (edge_r, flat_r, rhs_r))):
        for dx, first, count in ((-1, 0, WIDE), (0, WIDE, NX), (1, WIDE + NX, WIDE)):

            @pl.when(jnp.logical_not(there(dx, dy)))
            def _():
                for end in ends[:2]:
                    end[first : first + count, :] = jnp.zeros((count, 128), end.dtype)
                ends[2][:, first : first + count, :] = jnp.zeros((2, count, 128), F32)

    for tile, fine in enumerate((*range(FINE), -1, FINE)):
        place[:, 128 * tile : 128 * tile + 128] = chooser(fine)
    for lot in range(LOTS):
        back[:, 128 * lot : 128 * lot + 128] = returner(lot)

    pl.semaphore_wait(barrier, met)

    swap = [
        pltpu.make_async_remote_copy(
            visc_ref.at[:, :, other_cols],
            visc.at[mine, own_rows],
            swap_send.at[0],
            swap_recv.at[0],
            device_id=partner,
            device_id_type=MESH,
        ),
        pltpu.make_async_remote_copy(
            vel_ref.at[:, 0, :, other_cols],
            base.at[gz],
            swap_send.at[1],
            swap_recv.at[1],
            device_id=partner,
            device_id_type=MESH,
        ),
    ]
    for copy in swap:
        copy.start()

    for copy in local[1:]:
        copy.wait()

    lane = lanes_of((NX, NY))
    left_class, right_class = classes[0, 2 * gz], classes[0, 2 * gz + 1]
    kinds = jnp.where(lane < NY // 2, left_class, right_class)
    ice = (kinds > 0).astype(F32)
    friction = jnp.exp(logf[...]) * (kinds == 2).astype(F32) * contact[...].astype(F32)
    marked = jnp.where(kinds > 0, jnp.maximum(friction, 1e-30), 0.0)
    flat[2, own_rows, :] = marked

    swap[1].wait()
    drive = -(friction * step[...])
    flat[0, own_rows, :] = drive * base[0, 0].astype(F32)
    flat[1, own_rows, :] = drive * base[0, 1].astype(F32)

    def with_edges(packed, field, shift):
        for at, first in ((R_AT - shift, 0), (L_AT - shift, NY - WIDE)):
            packed = jnp.where((lane >= at) & (lane < at + WIDE), turned(field, at - first), packed)
        return packed

    packed = jnp.zeros((NX, 128), F32)
    for i in range(3):
        packed = with_edges(packed, flat[i, own_rows, :], 32 - 16 * i)
    flat_pack[...] = packed

    def extent(dx):
        if dx == 0:
            return pl.ds(WIDE, NX), pl.ds(0, NX), pl.ds(WIDE, NX)
        if dx < 0:
            return pl.ds(WIDE, WIDE), pl.ds(0, WIDE), pl.ds(WIDE + NX, WIDE)
        return pl.ds(NX, WIDE), pl.ds(NX - WIDE, WIDE), pl.ds(0, WIDE)

    def to_neighbours(block, packs, lands, send, recv):
        copies = []
        for i, (dx, dy) in enumerate(DIRS):
            src, src_pack, dst = extent(dx)
            if dy == 0:
                pair = (block.at[:, src, :], block.at[:, dst, :])
            elif dy < 0:
                pair = (packs[0].at[src_pack, :], lands[1].at[dst, :])
            else:
                pair = (packs[1].at[src_pack, :], lands[0].at[dst, :])
            copies.append(
                pltpu.make_async_remote_copy(
                    *pair,
                    send.at[i],
                    recv.at[i],
                    device_id=device(dx, dy),
                    device_id_type=MESH,
                )
            )
        return copies

    def start_all(copies):
        for (dx, dy), copy in zip(DIRS, copies):
            pl.when(there(dx, dy))(copy.start)

    def arrived(copies):
        for (dx, dy), copy in zip(DIRS, copies):
            pl.when(there(-dx, -dy))(copy.wait_recv)

    def sent(copies):
        for (dx, dy), copy in zip(DIRS, copies):
            pl.when(there(dx, dy))(copy.wait_send)

    flat_copies = to_neighbours(flat, (flat_pack, flat_pack), (flat_l, flat_r), b_send, b_recv)
    start_all(flat_copies)

    local[0].wait()
    swap[0].wait()

    def pack_rows(i, _):
        rows = pl.ds(pl.multiple_of(i * 16, 16), 16)
        here = pl.ds(pl.multiple_of(WIDE + i * 16, 16), 16)
        spot = lanes_of((16, 128))
        low = jnp.zeros((16, 128), F32)
        high = jnp.zeros((16, 128), F32)
        for layer in range(NZ):
            e = visc[layer, here, :].astype(F32)
            inside = (spot >= 16 * layer) & (spot < 16 * layer + 16)
            low = jnp.where(inside, turned(e, 16 * layer), low)
            high = jnp.where(inside, turned(e, 16 * layer + 16), high)
        pack_l[rows, :] = low.astype(BF16)
        pack_r[rows, :] = high.astype(BF16)
        return 0

    lax.fori_loop(0, NX // 16, pack_rows, 0)
    visc_copies = to_neighbours(visc, (pack_l, pack_r), (edge_l, edge_r), a_send, a_recv)
    start_all(visc_copies)

    arrived(flat_copies)
    arrived(visc_copies)

    spot = lanes_of((XT, 128))

    def in_lots(own, edge):
        return jnp.concatenate(
            [part[ROWS * lot : ROWS * lot + ROWS] for lot in range(LOTS) for part in (own, edge)], axis=1
        )

    ends_l, ends_r = edge_l[...].astype(F32), edge_r[...].astype(F32)
    for layer in range(NZ):
        edge = jnp.where(spot < 64, turned(ends_r, R_AT - 16 * layer), turned(ends_l, L_AT - 16 * layer))
        left[ROWS * layer : ROWS * layer + ROWS, :] = in_lots(visc[layer].astype(F32), edge)

    tiles = FINE + 2
    rows_in = left[...].astype(BF16)
    for tile in range(tiles):
        placed = 0.5 * dot(rows_in, place[:, 128 * tile : 128 * tile + 128])
        for layer in range(NZ):
            e_buf[pl.ds(tiles * NZ + tile * NZ + layer, ROWS, stride=tiles * NZ), :] = placed[
                ROWS * layer : ROWS * layer + ROWS
            ]

    def e_tile(row, tile):
        return pl.ds(pl.multiple_of((row * tiles + tile) * NZ, NZ), NZ)

    for fine in range(FINE):
        e_buf[e_tile(0, fine), :] = pltpu.roll(e_buf[e_tile(ROWS, fine), :], BLOCKS, 1)
        e_buf[e_tile(ROWS + 1, fine), :] = pltpu.roll(e_buf[e_tile(1, fine), :], 128 - BLOCKS, 1)

    def put(i, placed):
        for fine in range(FINE):
            spread[i, fine] = placed[:, 128 * fine : 128 * fine + 128]

    ends = jnp.where(spot < 48, flat_r[...], flat_l[...])
    flat_rows = jnp.concatenate([in_lots(flat[i], turned(ends, 32 - 16 * i)) for i in range(3)], axis=0)
    placed = exact_dot(flat_rows, place[:, : 128 * FINE])
    for i in range(3):
        put(i, placed[ROWS * i : ROWS * i + ROWS])

    level = lax.broadcasted_iota(jnp.int32, (NZ, 128), 0)

    def flat_tile(i, q, fine):
        return jnp.broadcast_to(spread[i, fine, pl.ds(q, 1), :], (NZ, 128))

    def faces(q, _):
        for fine in range(FINE):
            here = e_buf[e_tile(q + 1, fine), :]

            def side(beside):
                return here + jnp.where(beside > 0, beside, here)

            def column(beside):
                return ASPECT * (here + beside)

            marks = flat_tile(2, q, fine)
            parts = [
                side(e_buf[e_tile(q, fine), :]),
                side(e_buf[e_tile(q + 2, fine), :]),
                side(e_buf[e_tile(q + 1, fine - 1 if fine else FINE), :]),
                side(e_buf[e_tile(q + 1, fine + 1 if fine < FINE - 1 else FINE + 1), :]),
                jnp.where(level > 0, column(pltpu.roll(here, 1, 0)), 0.0),
                jnp.where(level < NZ - 1, column(pltpu.roll(here, NZ - 1, 0)), 0.0),
            ]
            total = parts[0] + parts[1] + parts[2] + parts[3] + parts[4] + parts[5]
            total = total + jnp.where(level == 0, marks, 0.0)
            inverse = jnp.where(marks > 0, 1.0 / jnp.where(marks > 0, total, 1.0), 0.0)
            for j, part in enumerate(parts):
                gs[q, fine, j] = part * inverse
            inv[q, fine] = SCALE * inverse
        return 0

    lax.fori_loop(0, ROWS, faces, 0)

    def across(buf, row):
        return pltpu.roll(buf[row, FINE - 1], 1, 1), pltpu.roll(buf[row, 0], 127, 1)

    def apply(src, src_ext, dst, dst_ext, centre, shift):
        found = {q: across(src, q + 1) for q in ROW_ORDER if q in LATE}
        for q in ROW_ORDER:
            here = [src[q + 1, fine] for fine in range(FINE)]
            sides = found[q] if q in LATE else (src_ext[q, 0], src_ext[q, 1])
            row = []
            for fine in range(FINE):
                before = here[fine - 1] if fine else sides[0]
                after = here[fine + 1] if fine < FINE - 1 else sides[1]
                new = (
                    (gs[q, fine, 0] * src[q, fine] + gs[q, fine, 1] * src[q + 2, fine])
                    + (gs[q, fine, 2] * before + gs[q, fine, 3] * after)
                    + (
                        gs[q, fine, 4] * pltpu.roll(here[fine], 1, 0)
                        + gs[q, fine, 5] * pltpu.roll(here[fine], NZ - 1, 0)
                    )
                )
                new = new + shift * (here[fine] if centre is src else centre[q + 1, fine])
                dst[q + 1, fine] = new
                row.append(new)
            if q not in LATE:
                dst_ext[q, 0], dst_ext[q, 1] = pltpu.roll(row[FINE - 1], 1, 1), pltpu.roll(row[0], 127, 1)
            if q == ROWS - 1:
                for fine in range(FINE):
                    dst[0, fine] = pltpu.roll(row[fine], BLOCKS, 1)
            if q == 0:
                for fine in range(FINE):
                    dst[ROWS + 1, fine] = pltpu.roll(row[fine], 128 - BLOCKS, 1)

    def pick(values, i):
        out = jnp.float32(values[0])
        for k in range(1, len(values)):
            out = jnp.where(i == k, jnp.float32(values[k]), out)
        return out

    def solve(i, floor_only):
        def start_rows(j, _):
            for m in range(4):
                q = 4 * j + m
                for fine in range(FINE):
                    value = inv[q, fine] * flat_tile(i, q, fine)
                    u_buf[q + 1, fine] = jnp.where((level == 0) | jnp.logical_not(floor_only), value, 0.0)
            return 0

        lax.fori_loop(0, ROWS // 4, start_rows, 0)
        for fine in range(FINE):
            u_buf[0, fine] = pltpu.roll(u_buf[ROWS, fine], BLOCKS, 1)
            u_buf[ROWS + 1, fine] = pltpu.roll(u_buf[1, fine], 128 - BLOCKS, 1)
        for q in range(ROWS):
            if q not in LATE:
                u_ext[q, 0], u_ext[q, 1] = across(u_buf, q + 1)

        apply(u_buf, u_ext, t_buf, t_ext, u_buf, jnp.float32(LINEAR))

        def factor(j, _):
            apply(t_buf, t_ext, u_buf, u_ext, t_buf, pick(PS, j))
            apply(u_buf, u_ext, t_buf, t_ext, t_buf, pick(QS, j))
            return 0

        lax.fori_loop(0, len(PS), factor, 0)

    def own_columns():
        out = exact_dot(jnp.concatenate([sums[fine] for fine in range(FINE)], axis=1), back[...])
        cut = [slice(WIDE, ROWS), slice(0, ROWS), slice(0, ROWS), slice(0, ROWS - WIDE)]
        return jnp.concatenate([out[rows, 128 * lot : 128 * lot + 128] for lot, rows in enumerate(cut)], axis=0)

    def fold(reduce):
        for q in range(ROWS):
            for fine in range(FINE):
                sums[fine, q : q + 1, :] = reduce(t_buf[q + 1, fine])

    weight = ice * obs[...]

    def rhs_copies(c):
        packs = rhs_pack.at[c]
        return to_neighbours(
            rhs.at[pl.ds(c, 1)], (packs, packs), (rhs_l.at[c], rhs_r.at[c]), c_send.at[c], c_recv.at[c]
        )

    def depth_copies(c):
        here = pltpu.make_async_copy(depth.at[c], depth_ref.at[c, :, own_cols], local_sem.at[8 + c])
        there_too = pltpu.make_async_remote_copy(
            depth.at[c],
            depth_ref.at[c, :, own_cols],
            swap_send.at[2 + c],
            swap_recv.at[2 + c],
            device_id=partner,
            device_id_type=MESH,
        )
        return here, there_too

    def phase(p, _):
        c = lax.rem(p, 2)
        forward = p < 2

        @pl.when(jnp.logical_not(forward))
        def _():
            arrived(rhs_copies(c))
            edge = jnp.where(spot < 64, rhs_r[c], rhs_l[c])
            put(c, exact_dot(in_lots(rhs[c], edge), place[:, : 128 * FINE]))

        solve(c, forward)

        @pl.when(forward)
        def _():
            fold(lambda tile: jnp.sum(tile, axis=0, keepdims=True))
            field = own_columns()
            depth[c] = field
            field = weight * field
            rhs[c, own_rows, :] = field
            rhs_pack[c] = with_edges(jnp.zeros((NX, 128), F32), field, 0)
            start_all(rhs_copies(c))
            for copy in depth_copies(c):
                copy.start()

        @pl.when(jnp.logical_not(forward))
        def _():
            fold(lambda tile: tile[0:1, :])
            mult[c] = own_columns()

        return 0

    lax.fori_loop(0, 4, phase, 0)

    hess[...] = -friction * (base[0, 0].astype(F32) * mult[0] + base[0, 1].astype(F32) * mult[1])
    hess_out = pltpu.make_async_copy(hess, hess_ref, local_sem.at[7])
    hess_out.start()

    for copies in (flat_copies, visc_copies, rhs_copies(0), rhs_copies(1)):
        sent(copies)
    for c in range(2):
        for copy in depth_copies(c):
            copy.wait()
    hess_out.wait()


def solution(mesh):
    gx_n, gy_n = mesh.shape["gx"], mesh.shape["gy"]

    def step(viscosity, velocity, log_friction, step_dir, obs_weight, tile_mask, contact):
        any_space = pl.BlockSpec(memory_space=pl.ANY)
        vmem, dma = pltpu.VMEM, pltpu.SemaphoreType.DMA
        nd = len(DIRS)
        return pl.pallas_call(
            functools.partial(kernel, gx_n, gy_n),
            out_shape=(
                jax.ShapeDtypeStruct((2, NX, 2 * NY), F32),
                jax.ShapeDtypeStruct((NX, NY), F32),
            ),
            in_specs=[any_space] * 7,
            out_specs=(any_space, any_space),
            scratch_shapes=[
                vmem((NZ, XT, NY), BF16),
                vmem((XT, 128), BF16),
                vmem((XT, 128), BF16),
                vmem((NX, 128), BF16),
                vmem((NX, 128), BF16),
                vmem((2, 2, NX, NY), BF16),
                vmem((NX, NY), F32),
                vmem((NX, NY), F32),
                vmem((NX, NY), F32),
                vmem((NX, NY), jnp.int32),
                vmem((3, XT, NY), F32),
                vmem((NX, 128), F32),
                vmem((XT, 128), F32),
                vmem((XT, 128), F32),
                vmem((2, XT, NY), F32),
                vmem((2, NX, 128), F32),
                vmem((2, XT, 128), F32),
                vmem((2, XT, 128), F32),
                vmem((2, NX, NY), F32),
                vmem((NX, NY), F32),
                vmem((2, NX, NY), F32),
                vmem((ROWS * NZ, 256 * LOTS), F32),
                vmem(((ROWS + 2) * (FINE + 2) * NZ, 128), F32),
                vmem((3, FINE, ROWS, 128), F32),
                vmem((FINE, ROWS, 128), F32),
                vmem((256 * LOTS, (FINE + 2) * 128), BF16),
                vmem((FINE * 128, 128 * LOTS), BF16),
                vmem((ROWS, FINE, 6, NZ, 128), F32),
                vmem((ROWS, FINE, NZ, 128), F32),
                vmem((ROWS, 2, NZ, 128), F32),
                vmem((ROWS, 2, NZ, 128), F32),
                vmem((ROWS + 2, FINE, NZ, 128), F32),
                vmem((ROWS + 2, FINE, NZ, 128), F32),
                pltpu.SMEM((1, 4), jnp.int32),
                dma((10,)),
                dma((4,)),
                dma((4,)),
                dma((nd,)),
                dma((nd,)),
                dma((nd,)),
                dma((nd,)),
                dma((2, nd)),
                dma((2, nd)),
            ],
            compiler_params=pltpu.CompilerParams(
                collective_id=0, has_side_effects=True, vmem_limit_bytes=67043328
            ),
        )(viscosity, velocity, log_friction, step_dir, obs_weight, contact, tile_mask)

    in_specs = (
        P("gz", "gx", "gy"),
        P(None, "gz", "gx", "gy"),
        P("gx", "gy"),
        P("gx", "gy"),
        P("gx", "gy"),
        P("gx", "gy"),
        P("gx", "gy"),
    )
    out_specs = (P(None, "gx", "gy"), P("gx", ("gy", "gz")))
    return jax.shard_map(step, mesh=mesh, in_specs=in_specs, out_specs=out_specs, check_vma=False)
```

time: 43.5 us -> 37 us (0.85)
  Pallas kernels: 40.5 us -> 34 us
    pallas_call x1, Pallas kernels: 40.5 us -> 34 us  [step(): pl.pallas_call(functools.partial(kernel, gx_n, gy_n), out_shape=(jax.Shap...]
where the time goes in v3:
time: 37 us; the launch traced here: 36.9 us
  Pallas kernels  34 us (92%)
  local copies, waits for them, and re-layouts  2.19 us (6%)
  between operations  0.65 us (2%)
    pallas_call x1, Pallas kernels, step(): pl.pallas_call(functools.partial(kernel, gx_n, gy_n), out_shape=(jax.Shap...  34 us
    unnamed x4, local copies, waits for them, and re-layouts  2.19 us

profile of v3, /device:TPU:103, one launch (start us, length us, event | category | flops | bytes accessed | tf_op | source)
XLA Modules:
  0.0 36.9 jit_solution(5762595035677230605)
XLA Ops:
  0.6 34.0 %shard_map.86 = (f32[2,64,256]{2,1,0:T(8,128)}, f32[64,128]{1,0:T(8,128)}) custom-call(bf16[4,64,256]{2,1,0:T(8,128)(2,1)} %visc_ref.1, bf16[2,4,64,256]{3,2,1,0:T(8,128)(2,1)} %vel_ref.1, f32[64,256]{1,0:T(8,128)} %logf_ref.1, f32[64,256]{1,0:T(8,128)} %step_ref.1, f32[64,256]{1,0:T(8,128)} %obs_ref.1, s32[64,256]{1,0:T(8,128)} %contact_ref.1, s32[1,4]{1,0:T(1,128)} %tile_ref.1), custom_call_target="tpu_custom_call" | custom-call | tf_op jit(solution)/shard_map/pallas_call | solution.py:549
  34.7 0.0 copy-start
  34.7 1.6 %copy.11 = f32[2,64,256]{2,1,0:T(8,128)} copy(f32[2,64,256]{2,1,0:T(8,128)} %get-tuple-element.4) | data formatting | bytes 262144
  36.3 0.0 copy-done
  36.3 0.6 %copy.12 = f32[64,128]{1,0:T(8,128)} copy(f32[64,128]{1,0:T(8,128)S(1)} %copy-done) | data formatting | bytes 65536
Async XLA Ops:
  34.7 1.6 %copy-start = (f32[64,128]{1,0:T(8,128)S(1)}, f32[64,128]{1,0:T(8,128)}, u32[]{:S(2)}) copy-start(f32[64,128]{1,0:T(8,128)} %get-tuple-element.5) | copy-start | bytes 98308

commit v4 on v3

--- a/solution.py
+++ b/solution.py
@@ -39,7 +39,7 @@
 ROWS = XT // LOTS
 BLOCKS = 128 // LOTS
 FINE = YT // BLOCKS
-DIRS = [(dx, dy) for dx in (-1, 0, 1) for dy in (-1, 0, 1) if (dx, dy) != (0, 0)]
+DIRS = [(-1, -1), (-1, 1), (1, -1), (1, 1), (-1, 0), (1, 0), (0, -1), (0, 1)]
 R_AT, L_AT = 32, 80
 ROW_ORDER = [ROWS - 1, *range(8), *range(ROWS - 2, 15, -1), *range(8, 16)]
 LATE = range(12, 16)
@@ -211,6 +211,18 @@
     for lot in range(LOTS):
         back[:, 128 * lot : 128 * lot + 128] = returner(lot)
 
+    for copy in local[1:]:
+        copy.wait()
+
+    lane = lanes_of((NX, NY))
+    left_class, right_class = classes[0, 2 * gz], classes[0, 2 * gz + 1]
+    kinds = jnp.where(lane < NY // 2, left_class, right_class)
+    ice = (kinds > 0).astype(F32)
+    friction = jnp.exp(logf[...]) * (kinds == 2).astype(F32) * contact[...].astype(F32)
+    marked = jnp.where(kinds > 0, jnp.maximum(friction, 1e-30), 0.0)
+    flat[2, own_rows, :] = marked
+    drive = -(friction * step[...])
+
     pl.semaphore_wait(barrier, met)
 
     swap = [
@@ -234,31 +246,10 @@
     for copy in swap:
         copy.start()
 
-    for copy in local[1:]:
-        copy.wait()
-
-    lane = lanes_of((NX, NY))
-    left_class, right_class = classes[0, 2 * gz], classes[0, 2 * gz + 1]
-    kinds = jnp.where(lane < NY // 2, left_class, right_class)
-    ice = (kinds > 0).astype(F32)
-    friction = jnp.exp(logf[...]) * (kinds == 2).astype(F32) * contact[...].astype(F32)
-    marked = jnp.where(kinds > 0, jnp.maximum(friction, 1e-30), 0.0)
-    flat[2, own_rows, :] = marked
-
-    swap[1].wait()
-    drive = -(friction * step[...])
-    flat[0, own_rows, :] = drive * base[0, 0].astype(F32)
-    flat[1, own_rows, :] = drive * base[0, 1].astype(F32)
-
     def with_edges(packed, field, shift):
         for at, first in ((R_AT - shift, 0), (L_AT - shift, NY - WIDE)):
             packed = jnp.where((lane >= at) & (lane < at + WIDE), turned(field, at - first), packed)
         return packed
-
-    packed = jnp.zeros((NX, 128), F32)
-    for i in range(3):
-        packed = with_edges(packed, flat[i, own_rows, :], 32 - 16 * i)
-    flat_pack[...] = packed
 
     def extent(dx):
         if dx == 0:
@@ -300,32 +291,31 @@
         for (dx, dy), copy in zip(DIRS, copies):
             pl.when(there(dx, dy))(copy.wait_send)
 
+    local[0].wait()
+    swap[0].wait()
+
+    low = jnp.zeros((NX, 128), F32)
+    high = jnp.zeros((NX, 128), F32)
+    for layer in range(NZ):
+        e = visc[layer, own_rows, :].astype(F32)
+        inside = (lane >= 16 * layer) & (lane < 16 * layer + 16)
+        low = jnp.where(inside, turned(e, 16 * layer), low)
+        high = jnp.where(inside, turned(e, 16 * layer + 16), high)
+    pack_l[...] = low.astype(BF16)
+    pack_r[...] = high.astype(BF16)
+    visc_copies = to_neighbours(visc, (pack_l, pack_r), (edge_l, edge_r), a_send, a_recv)
+    start_all(visc_copies)
+
+    swap[1].wait()
+    flat[0, own_rows, :] = drive * base[0, 0].astype(F32)
+    flat[1, own_rows, :] = drive * base[0, 1].astype(F32)
+    packed = jnp.zeros((NX, 128), F32)
+    for i in range(3):
+        packed = with_edges(packed, flat[i, own_rows, :], 32 - 16 * i)
+    flat_pack[...] = packed
     flat_copies = to_neighbours(flat, (flat_pack, flat_pack), (flat_l, flat_r), b_send, b_recv)
     start_all(flat_copies)
 
-    local[0].wait()
-    swap[0].wait()
-
-    def pack_rows(i, _):
-        rows = pl.ds(pl.multiple_of(i * 16, 16), 16)
-        here = pl.ds(pl.multiple_of(WIDE + i * 16, 16), 16)
-        spot = lanes_of((16, 128))
-        low = jnp.zeros((16, 128), F32)
-        high = jnp.zeros((16, 128), F32)
-        for layer in range(NZ):
-            e = visc[layer, here, :].astype(F32)
-            inside = (spot >= 16 * layer) & (spot < 16 * layer + 16)
-            low = jnp.where(inside, turned(e, 16 * layer), low)
-            high = jnp.where(inside, turned(e, 16 * layer + 16), high)
-        pack_l[rows, :] = low.astype(BF16)
-        pack_r[rows, :] = high.astype(BF16)
-        return 0
-
-    lax.fori_loop(0, NX // 16, pack_rows, 0)
-    visc_copies = to_neighbours(visc, (pack_l, pack_r), (edge_l, edge_r), a_send, a_recv)
-    start_all(visc_copies)
-
-    arrived(flat_copies)
     arrived(visc_copies)
 
     spot = lanes_of((XT, 128))
@@ -360,6 +350,7 @@
         for fine in range(FINE):
             spread[i, fine] = placed[:, 128 * fine : 128 * fine + 128]
 
+    arrived(flat_copies)
     ends = jnp.where(spot < 48, flat_r[...], flat_l[...])
     flat_rows = jnp.concatenate([in_lots(flat[i], turned(ends, 32 - 16 * i)) for i in range(3)], axis=0)
     placed = exact_dot(flat_rows, place[:, : 128 * FINE])
@@ -371,8 +362,9 @@
     def flat_tile(i, q, fine):
         return jnp.broadcast_to(spread[i, fine, pl.ds(q, 1), :], (NZ, 128))
 
-    def faces(q, _):
-        for fine in range(FINE):
+    def faces(i, _):
+        for k in range(2 * FINE):
+            q, fine = 2 * i + k // FINE, k % FINE
             here = e_buf[e_tile(q + 1, fine), :]
 
             def side(beside):
@@ -398,16 +390,19 @@
             inv[q, fine] = SCALE * inverse
         return 0
 
-    lax.fori_loop(0, ROWS, faces, 0)
+    lax.fori_loop(0, ROWS // 2, faces, 0)
 
     def across(buf, row):
         return pltpu.roll(buf[row, FINE - 1], 1, 1), pltpu.roll(buf[row, 0], 127, 1)
 
     def apply(src, src_ext, dst, dst_ext, centre, shift):
-        found = {q: across(src, q + 1) for q in ROW_ORDER if q in LATE}
+        found = {q: across(src, q + 1) for q in ROW_ORDER if q in LATE and src_ext is not None}
         for q in ROW_ORDER:
             here = [src[q + 1, fine] for fine in range(FINE)]
-            sides = found[q] if q in LATE else (src_ext[q, 0], src_ext[q, 1])
+            if src_ext is None:
+                sides = across(src, q + 1)
+            else:
+                sides = found[q] if q in LATE else (src_ext[q, 0], src_ext[q, 1])
             row = []
             for fine in range(FINE):
                 before = here[fine - 1] if fine else sides[0]
@@ -451,11 +446,8 @@
         for fine in range(FINE):
             u_buf[0, fine] = pltpu.roll(u_buf[ROWS, fine], BLOCKS, 1)
             u_buf[ROWS + 1, fine] = pltpu.roll(u_buf[1, fine], 128 - BLOCKS, 1)
-        for q in range(ROWS):
-            if q not in LATE:
-                u_ext[q, 0], u_ext[q, 1] = across(u_buf, q + 1)
-
-        apply(u_buf, u_ext, t_buf, t_ext, u_buf, jnp.float32(LINEAR))
+
+        apply(u_buf, None, t_buf, t_ext, u_buf, jnp.float32(LINEAR))
 
         def factor(j, _):
             apply(t_buf, t_ext, u_buf, u_ext, t_buf, pick(PS, j))

time: 37 us -> 36.4 us (0.984)
  Pallas kernels: 34 us -> 33.4 us
    pallas_call x1, Pallas kernels: 34 us -> 33.4 us  [step(): pl.pallas_call(functools.partial(kernel, gx_n, gy_n), out_shape=(jax.Shap...]
where the time goes in v4:
time: 36.4 us; the launch traced here: 36.3 us
  Pallas kernels  33.4 us (92%)
  local copies, waits for them, and re-layouts  2.19 us (6%)
  between operations  0.65 us (2%)
    pallas_call x1, Pallas kernels, step(): pl.pallas_call(functools.partial(kernel, gx_n, gy_n), out_shape=(jax.Shap...  33.4 us
    unnamed x4, local copies, waits for them, and re-layouts  2.19 us

profile of v4, /device:TPU:103, one launch (start us, length us, event | category | flops | bytes accessed | tf_op | source)
XLA Modules:
  0.0 36.3 jit_solution(2179658714676962988)
XLA Ops:
  0.6 33.4 %shard_map.86 = (f32[2,64,256]{2,1,0:T(8,128)}, f32[64,128]{1,0:T(8,128)}) custom-call(bf16[4,64,256]{2,1,0:T(8,128)(2,1)} %visc_ref.1, bf16[2,4,64,256]{3,2,1,0:T(8,128)(2,1)} %vel_ref.1, f32[64,256]{1,0:T(8,128)} %logf_ref.1, f32[64,256]{1,0:T(8,128)} %step_ref.1, f32[64,256]{1,0:T(8,128)} %obs_ref.1, s32[64,256]{1,0:T(8,128)} %contact_ref.1, s32[1,4]{1,0:T(1,128)} %tile_ref.1), custom_call_target="tpu_custom_call" | custom-call | tf_op jit(solution)/shard_map/pallas_call | solution.py:541
  34.1 0.0 copy-start
  34.1 1.6 %copy.11 = f32[2,64,256]{2,1,0:T(8,128)} copy(f32[2,64,256]{2,1,0:T(8,128)} %get-tuple-element.4) | data formatting | bytes 262144
  35.6 0.0 copy-done
  35.6 0.6 %copy.12 = f32[64,128]{1,0:T(8,128)} copy(f32[64,128]{1,0:T(8,128)S(1)} %copy-done) | data formatting | bytes 65536
Async XLA Ops:
  34.1 1.6 %copy-start = (f32[64,128]{1,0:T(8,128)S(1)}, f32[64,128]{1,0:T(8,128)}, u32[]{:S(2)}) copy-start(f32[64,128]{1,0:T(8,128)} %get-tuple-element.5) | copy-start | bytes 98308

commit v5 on v4

--- a/solution.py
+++ b/solution.py
@@ -592,9 +592,14 @@
                 dma((2, nd)),
             ],
             compiler_params=pltpu.CompilerParams(
-                collective_id=0, has_side_effects=True, vmem_limit_bytes=67043328
+                collective_id=0, has_side_effects=True, vmem_limit_bytes=40 * 1024 * 1024
             ),
-        )(viscosity, velocity, log_friction, step_dir, obs_weight, contact, tile_mask)
+        )(
+            *(
+                pltpu.with_memory_space_constraint(x, pltpu.HBM)
+                for x in (viscosity, velocity, log_friction, step_dir, obs_weight, contact, tile_mask)
+            )
+        )
 
     in_specs = (
         P("gz", "gx", "gy"),

time: 36.4 us -> 35 us (0.962)
  local copies, waits for them, and re-layouts: 2.19 us -> 1.27 us
  Pallas kernels: 33.4 us -> 32.9 us
    unnamed x4 -> x2, local copies, waits for them, and re-layouts: 2.19 us -> 1.27 us
    pallas_call x1, Pallas kernels: 33.4 us -> 32.9 us  [step(): pl.pallas_call(functools.partial(kernel, gx_n, gy_n), out_shape=(jax.Shap...]
where the time goes in v5:
time: 35 us; the launch traced here: 34.8 us
  Pallas kernels  32.9 us (94%)
  local copies, waits for them, and re-layouts  1.27 us (4%)
  between operations  0.64 us (2%)
    pallas_call x1, Pallas kernels, step(): pl.pallas_call(functools.partial(kernel, gx_n, gy_n), out_shape=(jax.Shap...  32.9 us
    unnamed x2, local copies, waits for them, and re-layouts  1.27 us

profile of v5, /device:TPU:103, one launch (start us, length us, event | category | flops | bytes accessed | tf_op | source)
XLA Modules:
  0.0 34.8 jit_solution(14906014691808500177)
XLA Ops:
  0.6 32.9 %shard_map.86 = (f32[2,64,256]{2,1,0:T(8,128)S(1)}, f32[64,128]{1,0:T(8,128)S(1)}) custom-call(bf16[4,64,256]{2,1,0:T(8,128)(2,1)} %visc_ref.1, bf16[2,4,64,256]{3,2,1,0:T(8,128)(2,1)} %vel_ref.1, f32[64,256]{1,0:T(8,128)} %logf_ref.1, f32[64,256]{1,0:T(8,128)} %step_ref.1, f32[64,256]{1,0:T(8,128)} %obs_ref.1, s32[64,256]{1,0:T(8,128)} %contact_ref.1, ...), custom_call_target="tpu_custom_call" | custom-call | tf_op jit(solution)/shard_map/pallas_call | solution.py:541
  33.6 0.7 %copy.11 = f32[2,64,256]{2,1,0:T(8,128)} copy(f32[2,64,256]{2,1,0:T(8,128)S(1)} %get-tuple-element.4) | data formatting | bytes 262144
  34.2 0.6 %copy.12 = f32[64,128]{1,0:T(8,128)} copy(f32[64,128]{1,0:T(8,128)S(1)} %get-tuple-element.5) | data formatting | bytes 65536

commit v6 on v5

--- a/solution.py
+++ b/solution.py
@@ -119,7 +119,6 @@
     rhs_l,
     rhs_r,
     depth,
-    hess,
     mult,
     left,
     e_buf,
@@ -519,16 +518,24 @@
 
     lax.fori_loop(0, 4, phase, 0)
 
-    hess[...] = -friction * (base[0, 0].astype(F32) * mult[0] + base[0, 1].astype(F32) * mult[1])
-    hess_out = pltpu.make_async_copy(hess, hess_ref, local_sem.at[7])
-    hess_out.start()
+    hess_ref[...] = -friction * (base[0, 0].astype(F32) * mult[0] + base[0, 1].astype(F32) * mult[1])
 
     for copies in (flat_copies, visc_copies, rhs_copies(0), rhs_copies(1)):
         sent(copies)
     for c in range(2):
         for copy in depth_copies(c):
             copy.wait()
-    hess_out.wait()
+
+
+def hand_over(depth_in, hess_in, depth_out, hess_out, sem):
+    copies = [
+        pltpu.make_async_copy(depth_in, depth_out, sem.at[0]),
+        pltpu.make_async_copy(hess_in, hess_out, sem.at[1]),
+    ]
+    for copy in copies:
+        copy.start()
+    for copy in copies:
+        copy.wait()
 
 
 def solution(mesh):
@@ -538,14 +545,14 @@
         any_space = pl.BlockSpec(memory_space=pl.ANY)
         vmem, dma = pltpu.VMEM, pltpu.SemaphoreType.DMA
         nd = len(DIRS)
-        return pl.pallas_call(
+        results = pl.pallas_call(
             functools.partial(kernel, gx_n, gy_n),
             out_shape=(
                 jax.ShapeDtypeStruct((2, NX, 2 * NY), F32),
                 jax.ShapeDtypeStruct((NX, NY), F32),
             ),
             in_specs=[any_space] * 7,
-            out_specs=(any_space, any_space),
+            out_specs=(any_space, pl.BlockSpec(memory_space=pltpu.VMEM)),
             scratch_shapes=[
                 vmem((NZ, XT, NY), BF16),
                 vmem((XT, 128), BF16),
@@ -566,7 +573,6 @@
                 vmem((2, XT, 128), F32),
                 vmem((2, XT, 128), F32),
                 vmem((2, NX, NY), F32),
-                vmem((NX, NY), F32),
                 vmem((2, NX, NY), F32),
                 vmem((ROWS * NZ, 256 * LOTS), F32),
                 vmem(((ROWS + 2) * (FINE + 2) * NZ, 128), F32),
@@ -600,6 +606,14 @@
                 for x in (viscosity, velocity, log_friction, step_dir, obs_weight, contact, tile_mask)
             )
         )
+        return pl.pallas_call(
+            hand_over,
+            out_shape=tuple(jax.ShapeDtypeStruct(x.shape, x.dtype) for x in results),
+            in_specs=[any_space, any_space],
+            out_specs=(any_space, any_space),
+            scratch_shapes=[dma((2,))],
+            compiler_params=pltpu.CompilerParams(vmem_limit_bytes=1024 * 1024),
+        )(*results)
 
     in_specs = (
         P("gz", "gx", "gy"),

time: 35 us -> 34.3 us (0.980)
  local copies, waits for them, and re-layouts: 1.27 us -> 0 us
  Pallas kernels: 32.9 us -> 33.6 us
    unnamed x2 -> x0, local copies, waits for them, and re-layouts: 1.27 us -> none
    pallas_call x0 -> x1, Pallas kernels: none -> 0.68 us  [step(): pl.pallas_call(hand_over, out_shape=tuple((jax.ShapeDtypeStruct(x.shape,...]
where the time goes in v6:
time: 34.3 us; the launch traced here: 34.2 us
  Pallas kernels  33.6 us (98%)
  between operations  0.64 us (2%)
    pallas_call x1, Pallas kernels, step(): pl.pallas_call(functools.partial(kernel, gx_n, gy_n), out_shape=(jax.Shap...  32.9 us

profile of v6, /device:TPU:103, one launch (start us, length us, event | category | flops | bytes accessed | tf_op | source)
XLA Modules:
  0.0 34.2 jit_solution(6052842747047784682)
XLA Ops:
  0.6 32.9 %shard_map.86 = (f32[2,64,256]{2,1,0:T(8,128)S(1)}, f32[64,128]{1,0:T(8,128)S(1)}) custom-call(bf16[4,64,256]{2,1,0:T(8,128)(2,1)} %visc_ref.1, bf16[2,4,64,256]{3,2,1,0:T(8,128)(2,1)} %vel_ref.1, f32[64,256]{1,0:T(8,128)} %logf_ref.1, f32[64,256]{1,0:T(8,128)} %step_ref.1, f32[64,256]{1,0:T(8,128)} %obs_ref.1, s32[64,256]{1,0:T(8,128)} %contact_ref.1, ...), custom_call_target="tpu_custom_call" | custom-call | tf_op jit(solution)/shard_map/pallas_call | solution.py:548
  33.5 0.7 %shard_map.87 = (f32[2,64,256]{2,1,0:T(8,128)}, f32[64,128]{1,0:T(8,128)}) custom-call(f32[2,64,256]{2,1,0:T(8,128)S(1)} %get-tuple-element.4.depth_in, f32[64,128]{1,0:T(8,128)S(1)} %get-tuple-element.5.hess_in), custom_call_target="tpu_custom_call" | custom-call | tf_op jit(solution)/shard_map/pallas_call | solution.py:609

commit v7 on v6

--- a/solution.py
+++ b/solution.py
@@ -315,6 +315,13 @@
     flat_copies = to_neighbours(flat, (flat_pack, flat_pack), (flat_l, flat_r), b_send, b_recv)
     start_all(flat_copies)
 
+    whole = [lot for lot in range(LOTS) if ROWS * lot >= WIDE and ROWS * (lot + 1) <= WIDE + NX]
+    for layer in range(NZ):
+        for lot in whole:
+            left[ROWS * layer : ROWS * layer + ROWS, 256 * lot : 256 * lot + 128] = visc[
+                layer, WIDE : WIDE + NX, :
+            ].astype(F32)[ROWS * lot - WIDE : ROWS * lot - WIDE + ROWS]
+
     arrived(visc_copies)
 
     spot = lanes_of((XT, 128))
@@ -327,7 +334,12 @@
     ends_l, ends_r = edge_l[...].astype(F32), edge_r[...].astype(F32)
     for layer in range(NZ):
         edge = jnp.where(spot < 64, turned(ends_r, R_AT - 16 * layer), turned(ends_l, L_AT - 16 * layer))
-        left[ROWS * layer : ROWS * layer + ROWS, :] = in_lots(visc[layer].astype(F32), edge)
+        own = visc[layer].astype(F32)
+        for lot in range(LOTS):
+            rows, here = slice(ROWS * lot, ROWS * lot + ROWS), slice(ROWS * layer, ROWS * layer + ROWS)
+            if lot not in whole:
+                left[here, 256 * lot : 256 * lot + 128] = own[rows]
+            left[here, 256 * lot + 128 : 256 * lot + 256] = edge[rows]
 
     tiles = FINE + 2
     rows_in = left[...].astype(BF16)
@@ -362,8 +374,8 @@
         return jnp.broadcast_to(spread[i, fine, pl.ds(q, 1), :], (NZ, 128))
 
     def faces(i, _):
-        for k in range(2 * FINE):
-            q, fine = 2 * i + k // FINE, k % FINE
+        for k in range(3 * FINE):
+            q, fine = 3 * i + k // FINE, k % FINE
             here = e_buf[e_tile(q + 1, fine), :]
 
             def side(beside):
@@ -389,7 +401,7 @@
             inv[q, fine] = SCALE * inverse
         return 0
 
-    lax.fori_loop(0, ROWS // 2, faces, 0)
+    lax.fori_loop(0, ROWS // 3, faces, 0)
 
     def across(buf, row):
         return pltpu.roll(buf[row, FINE - 1], 1, 1), pltpu.roll(buf[row, 0], 127, 1)
@@ -434,14 +446,14 @@
 
     def solve(i, floor_only):
         def start_rows(j, _):
-            for m in range(4):
-                q = 4 * j + m
+            for m in range(12):
+                q = 12 * j + m
                 for fine in range(FINE):
                     value = inv[q, fine] * flat_tile(i, q, fine)
                     u_buf[q + 1, fine] = jnp.where((level == 0) | jnp.logical_not(floor_only), value, 0.0)
             return 0
 
-        lax.fori_loop(0, ROWS // 4, start_rows, 0)
+        lax.fori_loop(0, ROWS // 12, start_rows, 0)
         for fine in range(FINE):
             u_buf[0, fine] = pltpu.roll(u_buf[ROWS, fine], BLOCKS, 1)
             u_buf[ROWS + 1, fine] = pltpu.roll(u_buf[1, fine], 128 - BLOCKS, 1)

time: 34.3 us -> 34.2 us (level)
  no operation moved by 1% of the time
where the time goes in v7:
time: 34.2 us; the launch traced here: 34.1 us
  Pallas kernels  33.5 us (98%)
  between operations  0.64 us (2%)
    pallas_call x1, Pallas kernels, step(): pl.pallas_call(functools.partial(kernel, gx_n, gy_n), out_shape=(jax.Shap...  32.8 us

profile of v7, /device:TPU:103, one launch (start us, length us, event | category | flops | bytes accessed | tf_op | source)
XLA Modules:
  0.0 34.1 jit_solution(15252325176197388150)
XLA Ops:
  0.6 32.8 %shard_map.86 = (f32[2,64,256]{2,1,0:T(8,128)S(1)}, f32[64,128]{1,0:T(8,128)S(1)}) custom-call(bf16[4,64,256]{2,1,0:T(8,128)(2,1)} %visc_ref.1, bf16[2,4,64,256]{3,2,1,0:T(8,128)(2,1)} %vel_ref.1, f32[64,256]{1,0:T(8,128)} %logf_ref.1, f32[64,256]{1,0:T(8,128)} %step_ref.1, f32[64,256]{1,0:T(8,128)} %obs_ref.1, s32[64,256]{1,0:T(8,128)} %contact_ref.1, ...), custom_call_target="tpu_custom_call" | custom-call | tf_op jit(solution)/shard_map/pallas_call | solution.py:560
  33.4 0.7 %shard_map.87 = (f32[2,64,256]{2,1,0:T(8,128)}, f32[64,128]{1,0:T(8,128)}) custom-call(f32[2,64,256]{2,1,0:T(8,128)S(1)} %get-tuple-element.4.depth_in, f32[64,128]{1,0:T(8,128)S(1)} %get-tuple-element.5.hess_in), custom_call_target="tpu_custom_call" | custom-call | tf_op jit(solution)/shard_map/pallas_call | solution.py:621

commit v8 on v7

--- a/solution.py
+++ b/solution.py
@@ -374,8 +374,8 @@
         return jnp.broadcast_to(spread[i, fine, pl.ds(q, 1), :], (NZ, 128))
 
     def faces(i, _):
-        for k in range(3 * FINE):
-            q, fine = 3 * i + k // FINE, k % FINE
+        for k in range(4 * FINE):
+            q, fine = 4 * i + k // FINE, k % FINE
             here = e_buf[e_tile(q + 1, fine), :]
 
             def side(beside):
@@ -401,7 +401,7 @@
             inv[q, fine] = SCALE * inverse
         return 0
 
-    lax.fori_loop(0, ROWS // 3, faces, 0)
+    lax.fori_loop(0, ROWS // 4, faces, 0)
 
     def across(buf, row):
         return pltpu.roll(buf[row, FINE - 1], 1, 1), pltpu.roll(buf[row, 0], 127, 1)
@@ -446,14 +446,14 @@
 
     def solve(i, floor_only):
         def start_rows(j, _):
-            for m in range(12):
-                q = 12 * j + m
+            for m in range(24):
+                q = 24 * j + m
                 for fine in range(FINE):
                     value = inv[q, fine] * flat_tile(i, q, fine)
                     u_buf[q + 1, fine] = jnp.where((level == 0) | jnp.logical_not(floor_only), value, 0.0)
             return 0
 
-        lax.fori_loop(0, ROWS // 12, start_rows, 0)
+        lax.fori_loop(0, ROWS // 24, start_rows, 0)
         for fine in range(FINE):
             u_buf[0, fine] = pltpu.roll(u_buf[ROWS, fine], BLOCKS, 1)
             u_buf[ROWS + 1, fine] = pltpu.roll(u_buf[1, fine], 128 - BLOCKS, 1)

time: 34.2 us -> 34.1 us (level)
  no operation moved by 1% of the time
where the time goes in v8:
time: 34.1 us; the launch traced here: 34 us
  Pallas kernels  33.3 us (98%)
  between operations  0.64 us (2%)
    pallas_call x1, Pallas kernels, step(): pl.pallas_call(functools.partial(kernel, gx_n, gy_n), out_shape=(jax.Shap...  32.6 us

profile of v8, /device:TPU:103, one launch (start us, length us, event | category | flops | bytes accessed | tf_op | source)
XLA Modules:
  0.0 34.0 jit_solution(15279632685294891615)
XLA Ops:
  0.6 32.6 %shard_map.86 = (f32[2,64,256]{2,1,0:T(8,128)S(1)}, f32[64,128]{1,0:T(8,128)S(1)}) custom-call(bf16[4,64,256]{2,1,0:T(8,128)(2,1)} %visc_ref.1, bf16[2,4,64,256]{3,2,1,0:T(8,128)(2,1)} %vel_ref.1, f32[64,256]{1,0:T(8,128)} %logf_ref.1, f32[64,256]{1,0:T(8,128)} %step_ref.1, f32[64,256]{1,0:T(8,128)} %obs_ref.1, s32[64,256]{1,0:T(8,128)} %contact_ref.1, ...), custom_call_target="tpu_custom_call" | custom-call | tf_op jit(solution)/shard_map/pallas_call | solution.py:560
  33.3 0.7 %shard_map.87 = (f32[2,64,256]{2,1,0:T(8,128)}, f32[64,128]{1,0:T(8,128)}) custom-call(f32[2,64,256]{2,1,0:T(8,128)S(1)} %get-tuple-element.4.depth_in, f32[64,128]{1,0:T(8,128)S(1)} %get-tuple-element.5.hess_in), custom_call_target="tpu_custom_call" | custom-call | tf_op jit(solution)/shard_map/pallas_call | solution.py:621
